TPU v7x, 512 devices: a whole 4x4x16 slice. The times are simulated.
512 devices in a mesh: gx: 64 (over z, x), gy: 8 (over y, core).
Axes of the slice: x: 4, y: 4, z: 16, core: 2. Of those that a mesh axis runs over, the one named last changes fastest.
Arguments:
- velocity: float32 [3, 512, 384, 256], P(None, 'gx', 'gy'), may hold values from -6 to 6
- pressure: float32 [512, 384, 256], P('gx', 'gy'), may hold values from -6 to 6
- viscosity: float32 [512, 384, 256], P('gx', 'gy'), may hold values from 0.12 to 0.6
- wind_profile: float32 [256], replicated, may hold values from 0.5 to 1.5
- panel_area: float32 [16384], P('gy'), may hold values from 0.5 to 2
- slot_cell: int32 [8, 4096], P('gy', 'gx'), may hold values from 0 to 98303
- slot_panel: int32 [8, 4096], P('gy'), may hold values from -1 to 2047, as said below
- panel_shapes: bfloat16 [16384, 2048], P('gy', 'gx'), may hold values from -0.046875 to 0.046875
- node_shapes: bfloat16 [1024, 2048], P(None, 'gx'), may hold values from -0.125 to 0.125
- damper_node: int32 [512], P('gy'), may hold values from 0 to 1022
- damper_viscous: float32 [512], P('gy'), may hold values from 0.2 to 2
- damper_hysteretic: float32 [512], P('gy'), may hold values from 0.2 to 2
- frequency: float32 [2048], P('gx'), may hold values from 0.2 to 1.8
- damping_ratio: float32 [2048], P('gx'), may hold values from 0.05 to 0.5
- modal_state: float32 [2, 2048], P(None, 'gx'), may hold values from -6 to 6
- damper_state: float32 [512], P('gy'), may hold values from -1 to 1
Outputs:
- velocity_next: float32 [3, 512, 384, 256], P(None, 'gx', 'gy')
- pressure_next: float32 [512, 384, 256], P('gx', 'gy')
- modal_next: float32 [2, 2048], P(None, 'gx')
- damper_next: float32 [512], P('gy')
Inputs may be any that keep to these rules, and one draw needn't show every extreme that they name: `slot_panel`: in every row each panel number 0 to 2047 stands in exactly one slot; every other slot holds -1.
All inputs are finite; a program needn't handle non-finite values.
Results may differ from a plain program's by a relative error of at most 0.0013.
Values may be sent and summed in bfloat16 or wider, within the bound.
A program may use at most 64 MiB of HBM per device.

v0:
```python
import jax
import jax.numpy as jnp
from jax import lax
from jax.sharding import PartitionSpec as P

time_step = 0.1
sound_squared = 1.0
modal_step = 0.5
hysteresis_gain = 1.0
shape_beta = 0.5
shape_gamma = 0.5
spring_rate = 0.5


def padded_2(value, sides, width):
    for axis, dim in sides:
        size, length = (lax.axis_size(axis), value.shape[dim])
        up = [(i, (i + 1) % size) for i in range(size - 1)]
        down = [(j, i) for i, j in up]
        last = lax.slice_in_dim(value, length - width, length, axis=dim)
        first = lax.slice_in_dim(value, 0, width, axis=dim)
        before = lax.ppermute(last, axis, up)
        after = lax.ppermute(first, axis, down)
        value = jnp.concatenate([before, value, after], axis=dim)
    return value


def advance(padded, local_viscosity, wind_profile):
    centre_cells = padded[:, 1:-1, 1:-1, 1:-1]
    ahead_cells = padded[:, 2:, 1:-1, 1:-1]
    behind_cells = padded[:, :-2, 1:-1, 1:-1]
    right_cells = padded[:, 1:-1, 2:, 1:-1]
    left_cells = padded[:, 1:-1, :-2, 1:-1]
    above_cells = padded[:, 1:-1, 1:-1, 2:]
    below_cells = padded[:, 1:-1, 1:-1, :-2]
    slope_stream = 0.5 * (ahead_cells - behind_cells)
    slope_span = 0.5 * (right_cells - left_cells)
    slope_vertical = 0.5 * (above_cells - below_cells)
    laplacian = (
        ahead_cells
        + behind_cells
        + right_cells
        + left_cells
        + above_cells
        + below_cells
        - 6.0 * centre_cells
    )
    pressure_slope = jnp.stack([slope_stream[3], slope_span[3], slope_vertical[3]])
    velocity_new = centre_cells[:3] + time_step * (
        -wind_profile * slope_stream[:3] + local_viscosity * laplacian[:3] - pressure_slope
    )
    pressure_new = centre_cells[3] - time_step * sound_squared * (
        slope_stream[0] + slope_span[1] + slope_vertical[2]
    )
    return jnp.concatenate([velocity_new, pressure_new[None]], axis=0)


def vertical_pad(fields):
    return jnp.pad(fields, ((0, 0), (0, 0), (0, 0), (1, 1)))


def body(
    velocity,
    pressure,
    viscosity,
    wind_profile,
    panel_area,
    slot_cell,
    slot_panel,
    panel_shapes,
    node_shapes,
    damper_node,
    damper_viscous,
    damper_hysteretic,
    frequency,
    damping_ratio,
    modal_state,
    damper_state,
):
    fields = jnp.concatenate([velocity, pressure[None]], axis=0)
    for substep in range(2):
        padded = padded_2(fields, (("gx", 1), ("gy", 2)), 1)
        fields = advance(vertical_pad(padded), viscosity, wind_profile)
    velocity_next = fields[:3]
    pressure_next = fields[3]
    slot_count = slot_cell.shape[1]
    panel_count = panel_area.shape[0]
    flat_pressure = pressure_next.reshape(-1)
    sampled = flat_pressure[slot_cell[0]]
    panel_ids = slot_panel[0]
    own_ids = lax.dynamic_slice_in_dim(panel_ids, lax.axis_index("gx") * slot_count, slot_count)
    safe_ids = jnp.where(own_ids < 0, 0, own_ids)
    own_loads = (panel_area[safe_ids] * sampled).astype(jnp.bfloat16)
    every_load = lax.all_gather(own_loads, "gx", axis=0, tiled=True)
    target = jnp.where(panel_ids < 0, panel_count, panel_ids)
    panel_loads = (
        jnp.zeros((panel_count + 1,), jnp.bfloat16).at[target].set(every_load)[:panel_count]
    )
    panel_part = jnp.dot(panel_loads, panel_shapes, preferred_element_type=jnp.float32)
    node_numbers = jnp.arange(node_shapes.shape[0], dtype=jnp.int32)
    upper_pick = (node_numbers[None, :] == damper_node[:, None] + 1).astype(jnp.float32)
    lower_pick = (node_numbers[None, :] == damper_node[:, None]).astype(jnp.float32)
    selector = (upper_pick - lower_pick).astype(jnp.bfloat16)
    drift_shapes = jnp.dot(selector, node_shapes, preferred_element_type=jnp.float32)
    panel_modal = lax.psum(panel_part, "gy")
    displacement = modal_state[0]
    modal_velocity = modal_state[1]
    hysteresis = damper_state
    for modal_turn in range(2):
        stretch, stretch_rate = lax.psum(
            (
                jnp.dot(drift_shapes, displacement, precision=lax.Precision.HIGHEST),
                jnp.dot(drift_shapes, modal_velocity, precision=lax.Precision.HIGHEST),
            ),
            "gx",
        )
        hysteresis = hysteresis + modal_step * (
            hysteresis_gain * stretch_rate
            - shape_beta * jnp.abs(stretch_rate) * hysteresis
            - shape_gamma * stretch_rate * jnp.abs(hysteresis)
        )
        damper_force = -(
            damper_viscous * stretch_rate + spring_rate * stretch + damper_hysteretic * hysteresis
        )
        generalized = jnp.dot(damper_force, drift_shapes, precision=lax.Precision.HIGHEST)
        modal_load = panel_modal + lax.psum(generalized, "gy")
        acceleration = (
            modal_load
            - 2.0 * damping_ratio * frequency * modal_velocity
            - frequency * frequency * displacement
        )
        modal_velocity = modal_velocity + modal_step * acceleration
        displacement = displacement + modal_step * modal_velocity
    return (velocity_next, pressure_next, jnp.stack([displacement, modal_velocity]), hysteresis)


def solution(mesh):
    placed = (
        P(None, "gx", "gy", None),
        P("gx", "gy", None),
        P("gx", "gy", None),
        P(),
        P("gy"),
        P("gy", "gx"),
        P("gy", None),
        P("gy", "gx"),
        P(None, "gx"),
        P("gy"),
        P("gy"),
        P("gy"),
        P("gx"),
        P("gx"),
        P(None, "gx"),
        P("gy"),
    )
    return jax.shard_map(
        body,
        mesh=mesh,
        in_specs=placed,
        out_specs=(P(None, "gx", "gy", None), P("gx", "gy", None), P(None, "gx"), P("gy")),
        check_vma=False,
    )
```

profile of v0, /device:TPU:1, one launch (start us, length us, event | category | flops | bytes accessed | tf_op | source)
XLA Modules:
  0.0 552.1 jit_solution(17609832479686283415)
XLA Ops:
  0.7 1.1 fusion.21
  1.9 4.0 collective-permute-start.1
  5.8 1.3 collective-permute-start
  8.4 3.8 collective-permute-done
  12.3 5.9 %collective-permute-start.3 = (f32[4,10,1,256]{3,2,1,0:T(1,128)S(1)}, f32[4,10,1,256]{3,2,1,0:T(1,128)S(1)}, u32[]{:S(2)}, u32[]{:S(2)}) collective-permute-start(f32[4,10,1,256]{3,2,1,0:T(1,128)S(1)} %get-tuple-element.38), channel_id=1, source_target_pairs={{0,1},{1,2},{2,3},{3,4},{4,5},{5,6},{6,7},{8,9},{9,10},{10,11},{11... | collective-permute-start | bytes 122888 | tf_op jit(solution)/shard_map/ppermute | solution.py:22
  18.2 2.7 collective-permute-start.2
  20.9 119.3 %all-reduce.4 = (f32[64]{0:T(128)S(1)}, f32[64]{0:T(128)S(1)}) all-reduce(f32[64]{0:T(128)S(1)} %convolution_bitcast_fusion.4, f32[64]{0:T(128)S(1)} %convolution_bitcast_fusion.5), channel_id=1, replica_groups=mesh['gx'=64,'gy'=8] {'gx'}, use_global_device_ids=true, to_apply=%region_3.4 | all-reduce | flops 128 | bytes 1024 | tf_op jit(solution)/shard_map/psum | solution.py:110
  140.2 3.5 select_maximum_fusion.5
  144.5 1.2 subtract_multiply_fusion.5
  145.9 0.9 copy-done.8
  147.4 1.2 fusion.13
  148.7 1.3 collective-permute-start.5
  150.0 1.3 collective-permute-start.4
  151.5 1.1 collective-permute-done.5
  152.6 3.8 collective-permute-done.4
  156.5 32.4 %collective-permute-start.7 = (f32[4,10,1,256]{3,2,1,0:T(1,128)S(1)}, f32[4,10,1,256]{3,2,1,0:T(1,128)S(1)}, u32[]{:S(2)}, u32[]{:S(2)}) collective-permute-start(f32[4,10,1,256]{3,2,1,0:T(1,128)S(1)} %get-tuple-element.33), channel_id=1, source_target_pairs={{0,1},{1,2},{2,3},{3,4},{4,5},{5,6},{6,7},{8,9},{9,10},{10,11},{11... | collective-permute-start | bytes 122888 | tf_op jit(solution)/shard_map/ppermute | solution.py:22
  188.9 1.9 collective-permute-start.6
  190.9 1.3 dynamic-slice.1
  194.2 3.5 select_maximum_fusion
  197.7 2.3 subtract_multiply_fusion
  200.8 3.0 subtract_multiply_fusion.2
  203.9 2.4 fusion.17
  207.0 0.9 copy.20
  208.0 1.8 gather_fusion.1
  210.0 112.8 %all-reduce.2 = bf16[4096]{0:T(1024)(128)(2,1)S(1)} all-reduce(bf16[4096]{0:T(1024)(128)(2,1)S(1)} %dynamic-update-slice), channel_id=1, replica_groups=mesh['gx'=64,'gy'=8] {'gx'}, use_global_device_ids=true, to_apply=%add.2 | all-reduce | flops 4096 | bytes 16384
  322.7 28.6 %scatter_custom_fusion = bf16[2049]{0:T(1024)(128)(2,1)S(1)} fusion(s32[4096]{0:T(1024)S(1)} %bitcast.100, bf16[4096]{0:T(1024)(128)(2,1)S(1)} %all-reduce.2, bf16[]{:T(256)} %constant.19.clone.1), kind=kCustom, calls=%fused_computation.120 | custom fusion | bytes 4100 | tf_op jit(solution)/shard_map/scatter | solution.py:97
  351.5 39.4 %all-reduce.5 = (f32[32]{0:T(128)S(1)}, f32[32]{0:T(128)S(1)}) all-reduce(f32[32]{0:T(128)S(1)} %convolution_bitcast_fusion.6, f32[32]{0:T(128)S(1)} %convolution_bitcast_fusion.3), channel_id=1, replica_groups=mesh['gx'=64,'gy'=8] {'gy'}, use_global_device_ids=true, to_apply=%region_1.2 | all-reduce | flops 64 | bytes 512 | tf_op jit(solution)/shard_map/psum | solution.py:105
  391.2 1.8 slice.229
  392.9 0.8 slice.228
  393.7 112.5 %all-reduce.3 = (f32[64]{0:T(128)S(1)}, f32[64]{0:T(128)S(1)}) all-reduce(f32[64]{0:T(128)S(1)} %convolution_bitcast_fusion.2, f32[64]{0:T(128)S(1)} %convolution_bitcast_fusion.1), channel_id=1, replica_groups=mesh['gx'=64,'gy'=8] {'gx'}, use_global_device_ids=true, to_apply=%region_5.6 | all-reduce | flops 128 | bytes 1024 | tf_op jit(solution)/shard_map/psum | solution.py:110
  506.4 39.4 %psum.55 = f32[32]{0:T(128)S(1)} all-reduce(f32[32]{0:T(128)S(1)} %convolution_bitcast_fusion), channel_id=1, replica_groups=mesh['gx'=64,'gy'=8] {'gy'}, use_global_device_ids=true, to_apply=%region_7.8 | all-reduce | flops 32 | bytes 256 | tf_op jit(solution)/shard_map/psum | solution.py:126
  546.4 5.7 %fusion.6 = f32[3,8,48,256]{3,2,1,0:T(8,128)} fusion(f32[3,8,48,256]{3,2,1,0:T(8,128)S(1)} %fusion.13, f32[4,8,48,256]{3,2,1,0:T(8,128)} %get-tuple-element.26, f32[1,8,48,256]{3,2,1,0:T(8,128)S(1)} %get-tuple-element.42, f32[4,8,48,256]{3,2,1,0:T(8,128)} %get-tuple-element.25, f32[4,8,48,256]{3,2,1,0:T(8,128)} %get-tuple-element.31, ...), kind=kLoop, calls=%fused_computation.60 | loop fusion | flops 4718592 | bytes 12583936 | tf_op jit(solution)/shard_map/add | solution.py:49
  (83 shorter events, 7.5 us)
Async XLA Ops:
  0.6 350.7 %copy-start = (bf16[2048,32]{0,1:T(8,128)(2,1)S(1)}, bf16[2048,32]{0,1:T(8,128)(2,1)}, u32[]{:S(2)}) copy-start(bf16[2048,32]{0,1:T(8,128)(2,1)} %param.23) | copy-start | bytes 393220
  0.6 11.6 %copy-start.2 = (f32[3,8,48,256]{3,2,1,0:T(8,128)S(1)}, f32[3,8,48,256]{3,2,1,0:T(8,128)}, u32[]{:S(2)}) copy-start(f32[3,8,48,256]{3,2,1,0:T(8,128)} %param.16) | copy-start | bytes 3538948
  0.7 11.6 %copy-start.3 = (f32[8,48,256]{2,1,0:T(8,128)S(1)}, f32[8,48,256]{2,1,0:T(8,128)}, u32[]{:S(2)}) copy-start(f32[8,48,256]{2,1,0:T(8,128)} %param.17) | copy-start | bytes 1179652
  0.7 6.5 %copy-start.22 = (s32[64]{0:T(128)S(1)}, s32[64]{0:T(128)}, u32[]{:S(2)}) copy-start(s32[64]{0:T(128)} %param.25) | copy-start | bytes 772
  0.7 6.5 %copy-start.21 = (bf16[1024,32]{0,1:T(8,128)(2,1)S(1)}, bf16[1024,32]{0,1:T(8,128)(2,1)}, u32[]{:S(2)}) copy-start(bf16[1024,32]{0,1:T(8,128)(2,1)} %param.24) | copy-start | bytes 196612
  0.7 6.7 %copy-start.12 = (f32[2,32]{1,0:T(2,128)S(1)}, f32[2,32]{1,0:T(2,128)}, u32[]{:S(2)}) copy-start(f32[2,32]{1,0:T(2,128)} %param.30) | copy-start | bytes 772
  0.7 7.0 %copy-start.13 = (s32[1,4096]{1,0:T(1,128)S(1)}, s32[1,4096]{1,0:T(1,128)}, u32[]{:S(2)}) copy-start(s32[1,4096]{1,0:T(1,128)} %param.22) | copy-start | bytes 49156
  0.7 7.0 %copy-start.23 = (s32[1,64]{1,0:T(1,128)S(1)}, s32[1,64]{1,0:T(1,128)}, u32[]{:S(2)}) copy-start(s32[1,64]{1,0:T(1,128)} %param.21) | copy-start | bytes 772
  1.9 19.1 %copy-start.20 = (f32[256]{0:T(256)S(1)}, f32[256]{0:T(256)}, u32[]{:S(2)}) copy-start(f32[256]{0:T(256)} %param.19) | copy-start | bytes 3076
  1.9 6.5 %collective-permute-start.1 = (f32[4,1,48,256]{3,2,1,0:T(8,128)S(1)}, f32[4,1,48,256]{3,2,1,0:T(8,128)S(1)}, u32[]{:S(2)}, u32[]{:S(2)}) collective-permute-start(f32[4,1,48,256]{3,2,1,0:T(8,128)S(1)} %get-tuple-element.46), channel_id=1, source_target_pairs={{0,8},{8,16},{16,24},{24,32},{32,40},{40,48},{48,56},{56,64},{64,7... | collective-permute-start | bytes 589832 | tf_op jit(solution)/shard_map/ppermute | solution.py:22
  5.8 6.4 %collective-permute-start = (f32[4,1,48,256]{3,2,1,0:T(8,128)S(1)}, f32[4,1,48,256]{3,2,1,0:T(8,128)S(1)}, u32[]{:S(2)}, u32[]{:S(2)}) collective-permute-start(f32[4,1,48,256]{3,2,1,0:T(8,128)S(1)} %get-tuple-element.47), channel_id=1, source_target_pairs={{8,0},{16,8},{24,16},{32,24},{40,32},{48,40},{56,48},{64,56},{72,6... | collective-permute-start | bytes 589832 | tf_op jit(solution)/shard_map/ppermute | solution.py:23
  12.3 127.9 %collective-permute-start.3 = (f32[4,10,1,256]{3,2,1,0:T(1,128)S(1)}, f32[4,10,1,256]{3,2,1,0:T(1,128)S(1)}, u32[]{:S(2)}, u32[]{:S(2)}) collective-permute-start(f32[4,10,1,256]{3,2,1,0:T(1,128)S(1)} %get-tuple-element.38), channel_id=1, source_target_pairs={{0,1},{1,2},{2,3},{3,4},{4,5},{5,6},{6,7},{8,9},{9,10},{10,11},{11... | collective-permute-start | bytes 122888 | tf_op jit(solution)/shard_map/ppermute | solution.py:22
  18.2 122.0 %collective-permute-start.2 = (f32[4,10,1,256]{3,2,1,0:T(1,128)S(1)}, f32[4,10,1,256]{3,2,1,0:T(1,128)S(1)}, u32[]{:S(2)}, u32[]{:S(2)}) collective-permute-start(f32[4,10,1,256]{3,2,1,0:T(1,128)S(1)} %get-tuple-element.39), channel_id=1, source_target_pairs={{1,0},{2,1},{3,2},{4,3},{5,4},{6,5},{7,6},{9,8},{10,9},{11,10},{12... | collective-permute-start | bytes 122888 | tf_op jit(solution)/shard_map/ppermute | solution.py:23
  144.4 1.2 copy-start.7
  145.6 1.2 copy-start.8
  145.6 1.7 copy-start.4
  145.7 1.7 copy-start.10
  148.6 2.8 copy-start.14
  148.6 2.8 copy-start.15
  148.6 2.8 copy-start.16
  148.6 44.1 %copy-start.1 = (f32[2048]{0:T(1024)S(1)}, f32[2048]{0:T(1024)}, u32[]{:S(2)}) copy-start(f32[2048]{0:T(1024)} %param.20) | copy-start | bytes 24580
  148.7 3.9 collective-permute-start.5
  150.0 6.4 %collective-permute-start.4 = (f32[4,1,48,256]{3,2,1,0:T(8,128)S(1)}, f32[4,1,48,256]{3,2,1,0:T(8,128)S(1)}, u32[]{:S(2)}, u32[]{:S(2)}) collective-permute-start(f32[4,1,48,256]{3,2,1,0:T(8,128)S(1)} %get-tuple-element.41), channel_id=1, source_target_pairs={{8,0},{16,8},{24,16},{32,24},{40,32},{48,40},{56,48},{64,56},{72,6... | collective-permute-start | bytes 589832 | tf_op jit(solution)/shard_map/ppermute | solution.py:23
  156.5 37.1 %collective-permute-start.7 = (f32[4,10,1,256]{3,2,1,0:T(1,128)S(1)}, f32[4,10,1,256]{3,2,1,0:T(1,128)S(1)}, u32[]{:S(2)}, u32[]{:S(2)}) collective-permute-start(f32[4,10,1,256]{3,2,1,0:T(1,128)S(1)} %get-tuple-element.33), channel_id=1, source_target_pairs={{0,1},{1,2},{2,3},{3,4},{4,5},{5,6},{6,7},{8,9},{9,10},{10,11},{11... | collective-permute-start | bytes 122888 | tf_op jit(solution)/shard_map/ppermute | solution.py:22
  188.9 5.3 collective-permute-start.6
  203.8 2.4 copy-start.5
  203.8 2.4 copy-start.9
  203.8 187.0 %copy-start.18 = (f32[32]{0:T(128)S(1)}, f32[32]{0:T(128)}, u32[]{:S(2)}) copy-start(f32[32]{0:T(128)} %param.28) | copy-start | bytes 388
  203.9 187.0 %copy-start.19 = (f32[32]{0:T(128)S(1)}, f32[32]{0:T(128)}, u32[]{:S(2)}) copy-start(f32[32]{0:T(128)} %param.29) | copy-start | bytes 388
  206.3 0.7 copy-start.11
  207.0 185.9 %copy-start.6 = (f32[4,8,48,256]{3,2,1,0:T(8,128)S(1)}, f32[4,8,48,256]{3,2,1,0:T(8,128)}, u32[]{:S(2)}) copy-start(f32[4,8,48,256]{3,2,1,0:T(8,128)} %copy-done.5) | copy-start | bytes 4718596
  506.2 45.8 %copy-start.17 = (f32[64]{0:T(128)}, f32[64]{0:T(128)S(1)}, u32[]{:S(2)}) copy-start(f32[64]{0:T(128)S(1)} %multiply_add_fusion.1) | copy-start | bytes 772
where the time goes:
time: 557 us; the launch traced here: 552 us
  blocking collectives  423 us (76%)
  starting transfers between devices  50.8 us (9%)
  local copies, waits for them, and re-layouts  39.3 us (7%)
  other arithmetic  25.7 us (5%)
  waiting for transfers between devices  10 us (2%)
    psum x2, blocking collectives, body(): lax.psum((jnp.dot(drift_shapes, displacement, precision=lax.Precision.HIG...  232 us
    unnamed x1, blocking collectives  113 us
    ppermute x4, starting transfers between devices, padded_2(): before = lax.ppermute(last, axis, up)  43.6 us
    psum x1, blocking collectives, body(): modal_load = panel_modal + lax.psum(generalized, 'gy')  39.4 us
    psum x1, blocking collectives, body(): panel_modal = lax.psum(panel_part, 'gy')  39.4 us
    scatter x1, local copies, waits for them, and re-layouts, body(): jnp.zeros((panel_count + 1,), jnp.bfloat16).at[target].set(every_load)  28.6 us
  transfers between devices with their start and end apart: 8, of which 5 were waited for; matrix products, arithmetic and copies ran while one was open for 1% of the time, Pallas kernels for 0%

commit v1 on v0

v1 whole, which is shorter than its diff:
```python
import jax
import jax.numpy as jnp
from jax import lax
from jax.experimental import pallas as pl
from jax.experimental.pallas import tpu as pltpu
from jax.sharding import PartitionSpec as P

time_step = 0.1
sound_squared = 1.0
modal_step = 0.5
hysteresis_gain = 1.0
shape_beta = 0.5
shape_gamma = 0.5
spring_rate = 0.5

CX, CY, NZ = 8, 48, 256
NGX, NGY = 64, 8
MB = 32
DB = 64
SL = 64
Y0 = 8
YT = CY // 8


def row_of(column, lane_shift=0, lanes=128):
    n = column.shape[0]
    sub = lax.broadcasted_iota(jnp.int32, (n, lanes), 0)
    lane = lax.broadcasted_iota(jnp.int32, (n, lanes), 1)
    return jnp.sum(jnp.where(lane == sub + lane_shift, column, 0.0), axis=0, keepdims=True)


def column_of(row, n, lane_shift=0):
    lanes = row.shape[1]
    sub = lax.broadcasted_iota(jnp.int32, (n, lanes), 0)
    lane = lax.broadcasted_iota(jnp.int32, (n, lanes), 1)
    zero = jnp.zeros((), row.dtype)
    return jnp.sum(jnp.where(lane == sub + lane_shift, row, zero), axis=1, keepdims=True)


def kernel(
    vel_h, pre_h, vis_h, wind, area, cell_s, cell_v, panels, shapes_t, nodes_t,
    dnode, dvisc, dhyst, freq, ratio, modal, dstate,
    vel_o, pre_o, modal_o, damp_o,
    f0, f1, vis, xs, xr, ys, yr, samp, onehot, lhs, g0, h1, g2, h3,
    in_sem, xss, xrs, yss, yrs, s_sem, r_sem,
):
    gx = lax.axis_index("gx")
    gy = lax.axis_index("gy")
    f32, bf16 = jnp.float32, jnp.bfloat16

    def gx_peer(k):
        return {"gx": lax.rem(gx + k, NGX)}

    def gy_peer(k):
        return {"gy": lax.rem(gy + k, NGY)}

    barrier = pltpu.get_barrier_semaphore()

    def greet_gx(k, carry):
        pl.semaphore_signal(barrier, 1, device_id=gx_peer(k))
        return carry

    def greet_gy(k, carry):
        pl.semaphore_signal(barrier, 1, device_id=gy_peer(k))
        return carry

    lax.fori_loop(1, NGX, greet_gx, 0)
    lax.fori_loop(1, NGY, greet_gy, 0)
    cv = pltpu.make_async_copy(vel_h, f0.at[0:3, 1 : 1 + CX, Y0 : Y0 + CY, :], in_sem.at[0])
    cp = pltpu.make_async_copy(pre_h, f0.at[3, 1 : 1 + CX, Y0 : Y0 + CY, :], in_sem.at[1])
    cn = pltpu.make_async_copy(vis_h, vis, in_sem.at[2])
    cv.start()
    cp.start()
    cn.start()
    cv.wait()
    cp.wait()

    y_order = (1, 0, 2, 3)

    def pack_x(f, p, comps):
        for k in comps:
            xs[p, 0, k] = f[k, CX, Y0 : Y0 + CY, :].astype(bf16)
            xs[p, 1, k] = f[k, 1, Y0 : Y0 + CY, :].astype(bf16)

    def pack_y(f, p, slots):
        for q in slots:
            k = y_order[q]
            for x in range(CX):
                ys[p, 0, q, x : x + 1, :] = f[k, x + 1, Y0 + CY - 1 : Y0 + CY, :]
                ys[p, 1, q, x : x + 1, :] = f[k, x + 1, Y0 : Y0 + 1, :]

    def x_copy(p, part, d, lo, hi):
        i = 2 * part + d
        return pltpu.make_async_remote_copy(
            xs.at[p, d, lo:hi], xr.at[p, d, lo:hi], xss.at[p, i], xrs.at[p, i],
            device_id=gx_peer(1 if d == 0 else NGX - 1),
        )

    def y_copy(p, part, d, lo, hi):
        i = 2 * part + d
        return pltpu.make_async_remote_copy(
            ys.at[p, d, lo:hi], yr.at[p, d, lo:hi], yss.at[p, i], yrs.at[p, i],
            device_id=gy_peer(1 if d == 0 else NGY - 1),
        )

    def unpack_x(f, p, comps):
        for k in comps:
            f[k, 0, Y0 : Y0 + CY, :] = jnp.where(gx == 0, 0.0, xr[p, 0, k].astype(f32))
            f[k, CX + 1, Y0 : Y0 + CY, :] = jnp.where(gx == NGX - 1, 0.0, xr[p, 1, k].astype(f32))

    def unpack_y(f, p, slots):
        for q in slots:
            k = y_order[q]
            for x in range(CX):
                f[k, x + 1, Y0 - 1 : Y0, :] = jnp.where(gy == 0, 0.0, yr[p, 0, q, x : x + 1, :])
                f[k, x + 1, Y0 + CY : Y0 + CY + 1, :] = jnp.where(
                    gy == NGY - 1, 0.0, yr[p, 1, q, x : x + 1, :]
                )

    pack_x(f0, 0, range(4))
    pack_y(f0, 0, range(4))
    pl.semaphore_wait(barrier, NGX - 1 + NGY - 1)
    hx1 = [x_copy(0, 0, d, 0, 4) for d in range(2)]
    hy1 = [y_copy(0, 0, d, 0, 4) for d in range(2)]
    for c in hy1 + hx1:
        c.start()

    dn = dnode[...]
    dn2 = jnp.concatenate([dn, dn], axis=1)
    node_no = lax.broadcasted_iota(jnp.int32, (nodes_t.shape[1], 2 * DB), 0)
    pick = jnp.where(node_no == dn2 + 1, 1.0, jnp.where(node_no == dn2, -1.0, 0.0)).astype(bf16)
    drift = jnp.dot(nodes_t[...], pick, preferred_element_type=f32)
    q0 = column_of(modal[0:1, :], MB)
    v0 = column_of(modal[1:2, :], MB)
    omega = column_of(freq[...], MB)
    zeta = column_of(ratio[...], MB)
    first_half = lax.broadcasted_iota(jnp.int32, (MB, 2 * DB), 1) < DB

    def stretch_row(q, v):
        return jnp.sum(drift * jnp.where(first_half, q, v), axis=0, keepdims=True)

    g0[gx, 1:2, :] = stretch_row(q0, v0)

    def table(i, carry):
        low = panels[pl.ds(i, 1), :] & 127
        sub = lax.broadcasted_iota(jnp.int32, (128, 128), 0)
        onehot[:, pl.ds(pl.multiple_of(i * 128, 128), 128)] = (sub == low).astype(f32).astype(bf16)
        return carry

    lax.fori_loop(0, panels.shape[0], table, 0)
    parity = lax.rem(gx, 2)
    own_ids = column_of(panels[pl.ds(gx // 2, 1), :], SL, SL * parity)
    panel_no = lax.broadcasted_iota(jnp.int32, (SL, area.shape[1]), 1)
    own_area = jnp.sum(jnp.where(panel_no == own_ids, area[...], 0.0), axis=1, keepdims=True)
    own_z = column_of(cell_v[...], SL) & (NZ - 1)
    z_mask = (lax.broadcasted_iota(jnp.int32, (SL, NZ), 1) == own_z)

    lane8 = lax.broadcasted_iota(jnp.int32, (8, NZ), 1)

    def above(v):
        return jnp.where(lane8 == NZ - 1, 0.0, pltpu.roll(v, NZ - 1, 1))

    def below(v):
        return jnp.where(lane8 == 0, 0.0, pltpu.roll(v, 1, 1))

    w_row = jnp.broadcast_to((-0.5 * time_step) * wind[...], (8, NZ))
    half = 0.5 * time_step

    def velocity_tile(f, x, t):
        rows = pl.ds(Y0 + 8 * t, 8)
        rows_m = pl.ds(Y0 + 8 * t - 1, 8)
        rows_p = pl.ds(Y0 + 8 * t + 1, 8)
        nu = time_step * vis[x - 1, 8 * t : 8 * t + 8, :]
        pc = f[3, x, rows, :]
        slope = (
            f[3, x + 1, rows, :] - f[3, x - 1, rows, :],
            f[3, x, rows_p, :] - f[3, x, rows_m, :],
            above(pc) - below(pc),
        )
        out = []
        for k in range(3):
            c = f[k, x, rows, :]
            a, b = f[k, x + 1, rows, :], f[k, x - 1, rows, :]
            r, l = f[k, x, rows_p, :], f[k, x, rows_m, :]
            u, d = above(c), below(c)
            lap = ((a + b) + (r + l)) + ((u + d) - 6.0 * c)
            out.append(c + (w_row * (a - b) + nu * lap - half * slope[k]))
        return out

    def pressure_tile(f, x, t):
        rows = pl.ds(Y0 + 8 * t, 8)
        rows_m = pl.ds(Y0 + 8 * t - 1, 8)
        rows_p = pl.ds(Y0 + 8 * t + 1, 8)
        w = f[2, x, rows, :]
        div = (f[0, x + 1, rows, :] - f[0, x - 1, rows, :]) + (
            (f[1, x, rows_p, :] - f[1, x, rows_m, :]) + (above(w) - below(w))
        )
        return f[3, x, rows, :] - (half * sound_squared) * div

    def first_layer(x, carry):
        for t in range(YT):
            rows = slice(Y0 + 8 * t, Y0 + 8 * t + 8)
            new = velocity_tile(f0, x, t)
            for k in range(3):
                f1[k, x, rows, :] = new[k]
            f1[3, x, rows, :] = pressure_tile(f0, x, t)
        return carry

    cn.wait()
    for c in hy1:
        c.wait_recv()
    unpack_y(f0, 0, range(4))
    lax.fori_loop(2, CX, first_layer, 0)
    for c in hx1:
        c.wait_recv()
    unpack_x(f0, 0, range(4))
    first_layer(1, 0)
    first_layer(CX, 0)

    pack_x(f1, 1, (0,))
    pack_y(f1, 1, (0,))
    hx2 = [x_copy(1, 0, d, 0, 1) for d in range(2)]
    hy2 = [y_copy(1, 0, d, 0, 1) for d in range(2)]
    for c in hx2 + hy2:
        c.start()
    pack_x(f1, 1, (1, 2, 3))
    pack_y(f1, 1, (1, 2, 3))
    hx3 = [x_copy(1, 1, d, 1, 4) for d in range(2)]
    hy3 = [y_copy(1, 1, d, 1, 4) for d in range(2)]
    for c in hx3 + hy3:
        c.start()
    for c in hx2 + hy2:
        c.wait_recv()
    unpack_x(f1, 1, (0,))
    unpack_y(f1, 1, (0,))

    def second_pressure(x, carry):
        for t in range(YT):
            pre_o[x - 1, 8 * t : 8 * t + 8, :] = pressure_tile(f1, x, t)
        return carry

    lax.fori_loop(1, CX + 1, second_pressure, 0)

    for s in range(SL):
        line = cell_s[0, s] >> 8
        plane = line // CY
        samp[s : s + 1, :] = pre_o[plane, pl.ds(line - plane * CY, 1), :]
    sampled = jnp.sum(jnp.where(z_mask, samp[...], 0.0), axis=1, keepdims=True)
    load = (own_area * sampled).astype(bf16).astype(f32)
    g0[gx, 0:1, :] = row_of(load, SL * parity)

    def all_gx(buf, sem_no):
        def send(k, carry):
            pltpu.make_async_remote_copy(
                buf.at[gx], buf.at[gx], s_sem.at[sem_no], r_sem.at[sem_no], device_id=gx_peer(k)
            ).start()
            return carry

        lax.fori_loop(1, NGX, send, 0)
        most = buf.at[pl.ds(0, NGX - 1)]
        return pltpu.make_async_remote_copy(
            most, most, s_sem.at[sem_no], r_sem.at[sem_no], device_id=gx_peer(1)
        )

    def all_gy(buf, sem_no):
        def send(k, carry):
            pltpu.make_async_remote_copy(
                buf.at[gy], buf.at[gy], s_sem.at[sem_no], r_sem.at[sem_no], device_id=gy_peer(k)
            ).start()
            return carry

        lax.fori_loop(1, NGY, send, 0)
        most = buf.at[pl.ds(0, NGY - 1)]
        return pltpu.make_async_remote_copy(
            most, most, s_sem.at[sem_no], r_sem.at[sem_no], device_id=gy_peer(1)
        )

    stage0 = all_gx(g0, 0)
    for c in hx3 + hy3:
        c.wait_recv()
    unpack_x(f1, 1, (1, 2, 3))
    unpack_y(f1, 1, (1, 2, 3))

    def second_velocity(x, carry):
        for t in range(YT):
            new = velocity_tile(f1, x, t)
            for k in range(3):
                vel_o[k, x - 1, 8 * t : 8 * t + 8, :] = new[k]
        return carry

    lax.fori_loop(1, CX + 1, second_velocity, 0)
    for c in hx1 + hy1 + hx2 + hy2 + hx3 + hy3:
        c.wait_send()

    stage0.wait_recv()
    sub16 = lax.broadcasted_iota(jnp.int32, (16, 128), 0)
    for i in range(NGX // 2):
        pair = g0[2 * i, 0:1, :] + g0[2 * i + 1, 0:1, :]
        high = panels[i : i + 1, :] >> 7
        lhs[:, i * 128 : (i + 1) * 128] = jnp.where(sub16 == high, pair, 0.0).astype(bf16)
    placed = lax.dot_general(
        lhs[...], onehot[...], (((1,), (1,)), ((), ())), preferred_element_type=f32
    )
    part = jnp.zeros((MB, 128), f32)
    for a in range(16):
        part = part + shapes_t[:, a * 128 : (a + 1) * 128].astype(f32) * placed[a : a + 1, :]
    panel_part = jnp.sum(part, axis=1, keepdims=True)

    def response(total, hysteresis):
        stretch = total[:, 0:DB]
        rate = total[:, DB : 2 * DB]
        hysteresis = hysteresis + modal_step * (
            hysteresis_gain * rate
            - shape_beta * jnp.abs(rate) * hysteresis
            - shape_gamma * rate * jnp.abs(hysteresis)
        )
        force = -(dvisc[...] * rate + spring_rate * stretch + dhyst[...] * hysteresis)
        return hysteresis, jnp.sum(drift[:, 0:DB] * force, axis=1, keepdims=True)

    hysteresis, damper_part = response(jnp.sum(g0[:, 1:2, :], axis=0), dstate[...])
    h1[gy] = row_of(panel_part) + row_of(damper_part, MB)
    stage1 = all_gy(h1, 1)
    stage0.wait_send()
    stage1.wait_recv()
    total1 = jnp.sum(h1[...], axis=0)
    panel_modal = column_of(total1, MB)

    def advance_modes(q, v, damper_load):
        acceleration = (
            panel_modal + damper_load - 2.0 * zeta * omega * v - omega * omega * q
        )
        v = v + modal_step * acceleration
        return q + modal_step * v, v

    q1, v1 = advance_modes(q0, v0, column_of(total1, MB, MB))
    g2[gx] = stretch_row(q1, v1)
    stage2 = all_gx(g2, 2)
    stage1.wait_send()
    stage2.wait_recv()
    hysteresis, damper_part = response(jnp.sum(g2[...], axis=0), hysteresis)
    damp_o[...] = hysteresis
    h3[gy] = row_of(damper_part)
    stage3 = all_gy(h3, 3)
    stage2.wait_send()
    stage3.wait_recv()
    q2, v2 = advance_modes(q1, v1, column_of(jnp.sum(h3[...], axis=0), MB))
    modal_o[0:1, :] = row_of(q2, 0, MB)
    modal_o[1:2, :] = row_of(v2, 0, MB)
    stage3.wait_send()


def body(
    velocity, pressure, viscosity, wind_profile, panel_area, slot_cell, slot_panel, panel_shapes,
    node_shapes, damper_node, damper_viscous, damper_hysteretic, frequency, damping_ratio,
    modal_state, damper_state,
):
    any_space = pl.BlockSpec(memory_space=pl.ANY)
    vmem = pl.BlockSpec(memory_space=pltpu.VMEM)
    smem = pl.BlockSpec(memory_space=pltpu.SMEM)
    f32, bf16 = jnp.float32, jnp.bfloat16
    slots = slot_panel.shape[1]
    vel, pre, modal, damp = pl.pallas_call(
        kernel,
        out_shape=(
            jax.ShapeDtypeStruct(velocity.shape, f32),
            jax.ShapeDtypeStruct(pressure.shape, f32),
            jax.ShapeDtypeStruct(modal_state.shape, f32),
            jax.ShapeDtypeStruct((1, DB), f32),
        ),
        in_specs=[any_space] * 3 + [vmem] * 2 + [smem] + [vmem] * 11,
        out_specs=(vmem,) * 4,
        scratch_shapes=[
            pltpu.VMEM((4, CX + 2, CY + 16, NZ), f32),
            pltpu.VMEM((4, CX + 2, CY + 16, NZ), f32),
            pltpu.VMEM((CX, CY, NZ), f32),
            pltpu.VMEM((2, 2, 4, CY, NZ), bf16),
            pltpu.VMEM((2, 2, 4, CY, NZ), bf16),
            pltpu.VMEM((2, 2, 4, CX, NZ), f32),
            pltpu.VMEM((2, 2, 4, CX, NZ), f32),
            pltpu.VMEM((SL, NZ), f32),
            pltpu.VMEM((128, slots), bf16),
            pltpu.VMEM((16, slots), bf16),
            pltpu.VMEM((NGX, 2, 128), f32),
            pltpu.VMEM((NGY, 1, 128), f32),
            pltpu.VMEM((NGX, 1, 128), f32),
            pltpu.VMEM((NGY, 1, 128), f32),
            pltpu.SemaphoreType.DMA((3,)),
            pltpu.SemaphoreType.DMA((2, 4)),
            pltpu.SemaphoreType.DMA((2, 4)),
            pltpu.SemaphoreType.DMA((2, 4)),
            pltpu.SemaphoreType.DMA((2, 4)),
            pltpu.SemaphoreType.DMA((4,)),
            pltpu.SemaphoreType.DMA((4,)),
        ],
        compiler_params=pltpu.CompilerParams(
            collective_id=0, has_side_effects=True, vmem_limit_bytes=40 << 20
        ),
    )(
        velocity, pressure, viscosity, wind_profile.reshape(1, -1), panel_area.reshape(1, -1),
        slot_cell, slot_cell, slot_panel.reshape(slots // 128, 128), panel_shapes.T, node_shapes.T,
        damper_node.reshape(1, -1), damper_viscous.reshape(1, -1), damper_hysteretic.reshape(1, -1),
        frequency.reshape(1, -1), damping_ratio.reshape(1, -1), modal_state,
        damper_state.reshape(1, -1),
    )
    return vel, pre, modal, damp.reshape(-1)


def solution(mesh):
    placed = (
        P(None, "gx", "gy", None),
        P("gx", "gy", None),
        P("gx", "gy", None),
        P(),
        P("gy"),
        P("gy", "gx"),
        P("gy", None),
        P("gy", "gx"),
        P(None, "gx"),
        P("gy"),
        P("gy"),
        P("gy"),
        P("gx"),
        P("gx"),
        P(None, "gx"),
        P("gy"),
    )
    return jax.shard_map(
        body,
        mesh=mesh,
        in_specs=placed,
        out_specs=(P(None, "gx", "gy", None), P("gx", "gy", None), P(None, "gx"), P("gy")),
        check_vma=False,
    )
```

time: 557 us -> 73 us (0.13)
  blocking collectives: 423 us -> 0 us
  Pallas kernels: 0 us -> 56.7 us
  starting transfers between devices: 50.8 us -> 0 us
  other arithmetic: 25.7 us -> 0 us
  local copies, waits for them, and re-layouts: 39.3 us -> 15.2 us
  waiting for transfers between devices: 10 us -> 0 us
    psum x4 -> x0, blocking collectives: 311 us -> none  [the longest x2 232 us: body(): lax.psum((jnp.dot(drift_shapes, displacement, precision=lax.Precision.HIG...]
    unnamed x1 -> x0, blocking collectives: 113 us -> none
    pallas_call x0 -> x1, Pallas kernels: none -> 56.7 us  [body(): pl.pallas_call(kernel, out_shape=(jax.ShapeDtypeStruct(velocity.shape, f3...]
    ppermute x8 -> x0, starting transfers between devices: 50.8 us -> none  [the longest x4 43.6 us: padded_2(): before = lax.ppermute(last, axis, up)]
    scatter x1 -> x0, local copies, waits for them, and re-layouts: 28.6 us -> none  [body(): jnp.zeros((panel_count + 1,), jnp.bfloat16).at[target].set(every_load)]
    unnamed x52 -> x36, local copies, waits for them, and re-layouts: 4.82 us -> 15.2 us
    ppermute x8 -> x0, waiting for transfers between devices: 10 us -> none  [the longest x4 8.32 us: padded_2(): after = lax.ppermute(first, axis, down)]
    concatenate x6 -> x0, other arithmetic: 8.27 us -> none  [the longest x4 7.11 us: padded_2(): value = jnp.concatenate([before, value, after], axis=dim)]
  transfers between devices with their start and end apart: 8 -> 0, of which waited for: 5 -> 0; matrix products, arithmetic and copies ran while one was open for 1% -> 0% of each run, Pallas kernels for 0% -> 0%
where the time goes in v1:
time: 73 us; the launch traced here: 72.5 us
  Pallas kernels  56.7 us (78%)
  local copies, waits for them, and re-layouts  15.2 us (21%)
    pallas_call x1, Pallas kernels, body(): pl.pallas_call(kernel, out_shape=(jax.ShapeDtypeStruct(velocity.shape, f3...  56.7 us
    unnamed x36, local copies, waits for them, and re-layouts  15.2 us

profile of v1, /device:TPU:1, one launch (start us, length us, event | category | flops | bytes accessed | tf_op | source)
XLA Modules:
  0.0 72.5 jit_solution(9257955856592598347)
XLA Ops:
  0.6 0.0 copy-start
  0.6 1.3 %copy-done = f32[3,8,48,256]{3,2,1,0:T(8,128)S(1)} copy-done((f32[3,8,48,256]{3,2,1,0:T(8,128)S(1)}, f32[3,8,48,256]{3,2,1,0:T(8,128)}, u32[]{:S(2)}) %copy-start) | copy-done | bytes 1179672
  1.9 0.0 copy-start.1
  1.9 1.0 %copy-done.1 = f32[8,48,256]{2,1,0:T(8,128)S(1)} copy-done((f32[8,48,256]{2,1,0:T(8,128)S(1)}, f32[8,48,256]{2,1,0:T(8,128)}, u32[]{:S(2)}) %copy-start.1) | copy-done | bytes 393240
  2.9 0.0 copy-start.2
  2.9 1.0 %copy-done.2 = f32[8,48,256]{2,1,0:T(8,128)S(1)} copy-done((f32[8,48,256]{2,1,0:T(8,128)S(1)}, f32[8,48,256]{2,1,0:T(8,128)}, u32[]{:S(2)}) %copy-start.2) | copy-done | bytes 393240
  3.9 0.0 copy-start.3
  3.9 0.9 %copy-done.3 = bf16[2048,32]{0,1:T(8,128)(2,1)S(1)} copy-done((bf16[2048,32]{0,1:T(8,128)(2,1)S(1)}, bf16[2048,32]{0,1:T(8,128)(2,1)}, u32[]{:S(2)}) %copy-start.3) | copy-done | bytes 131096
  4.8 0.0 copy-start.4
  4.8 0.8 %copy-done.4 = bf16[1024,32]{0,1:T(8,128)(2,1)S(1)} copy-done((bf16[1024,32]{0,1:T(8,128)(2,1)S(1)}, bf16[1024,32]{0,1:T(8,128)(2,1)}, u32[]{:S(2)}) %copy-start.4) | copy-done | bytes 65560
  5.6 0.0 copy-start.5
  5.6 0.7 copy-done.5
  6.4 0.7 copy-done.6
  7.1 0.0 copy-start.7
  7.1 0.7 copy-done.7
  7.7 0.0 copy-start.8
  7.7 0.7 copy-done.8
  8.4 0.0 copy-start.9
  8.4 0.7 copy-done.9
  9.1 0.0 copy-start.10
  9.1 0.7 copy-done.10
  9.7 0.0 copy-start.11
  9.7 0.7 copy-done.11
  10.4 0.7 copy-done.12
  11.0 0.7 copy-done.13
  11.7 0.7 copy-done.14
  12.4 0.7 copy-done.15
  13.0 56.7 %shard_map.183 = (f32[3,8,48,256]{3,2,1,0:T(8,128)S(1)}, f32[8,48,256]{2,1,0:T(8,128)S(1)}, f32[2,32]{1,0:T(2,128)S(1)}, f32[1,64]{1,0:T(1,128)S(1)}) custom-call(f32[3,8,48,256]{3,2,1,0:T(8,128)S(1)} %copy-done, f32[8,48,256]{2,1,0:T(8,128)S(1)} %copy-done.1, f32[8,48,256]{2,1,0:T(8,128)S(1)} %copy-done.2, f32[1,256]{1,0:T(1,128)S(1)} %bitcast.16, ...), custom_call_target="tpu_custom_call" | custom-call | tf_op jit(solution)/shard_map/pallas_call | solution.py:362
  69.7 1.0 %copy.24 = f32[3,8,48,256]{3,2,1,0:T(8,128)} copy(f32[3,8,48,256]{3,2,1,0:T(8,128)S(1)} %get-tuple-element.16) | data formatting | bytes 2359296
  70.7 0.7 %copy.25 = f32[8,48,256]{2,1,0:T(8,128)} copy(f32[8,48,256]{2,1,0:T(8,128)S(1)} %get-tuple-element.17) | data formatting | bytes 786432
  71.5 0.6 copy.26
  72.0 0.5 copy.27
  (5 shorter events, 0.0 us)
Async XLA Ops:
  0.6 1.3 %copy-start = (f32[3,8,48,256]{3,2,1,0:T(8,128)S(1)}, f32[3,8,48,256]{3,2,1,0:T(8,128)}, u32[]{:S(2)}) copy-start(f32[3,8,48,256]{3,2,1,0:T(8,128)} %vel_h.1) | copy-start | bytes 3538948
  1.9 1.0 %copy-start.1 = (f32[8,48,256]{2,1,0:T(8,128)S(1)}, f32[8,48,256]{2,1,0:T(8,128)}, u32[]{:S(2)}) copy-start(f32[8,48,256]{2,1,0:T(8,128)} %pre_h.1) | copy-start | bytes 1179652
  2.9 1.0 %copy-start.2 = (f32[8,48,256]{2,1,0:T(8,128)S(1)}, f32[8,48,256]{2,1,0:T(8,128)}, u32[]{:S(2)}) copy-start(f32[8,48,256]{2,1,0:T(8,128)} %vis_h.1) | copy-start | bytes 1179652
  3.9 0.9 %copy-start.3 = (bf16[2048,32]{0,1:T(8,128)(2,1)S(1)}, bf16[2048,32]{0,1:T(8,128)(2,1)}, u32[]{:S(2)}) copy-start(bf16[2048,32]{0,1:T(8,128)(2,1)} %param.23) | copy-start | bytes 393220
  4.8 0.8 %copy-start.4 = (bf16[1024,32]{0,1:T(8,128)(2,1)S(1)}, bf16[1024,32]{0,1:T(8,128)(2,1)}, u32[]{:S(2)}) copy-start(bf16[1024,32]{0,1:T(8,128)(2,1)} %param.24) | copy-start | bytes 196612
  5.6 0.7 copy-start.5
  6.4 0.7 copy-start.6
  7.1 0.7 copy-start.7
  7.7 0.7 copy-start.8
  8.4 0.7 copy-start.9
  9.1 0.7 copy-start.10
  9.7 0.7 copy-start.11
  10.4 0.7 copy-start.12
  11.0 0.7 copy-start.13
  11.7 0.7 copy-start.14
  12.4 0.7 copy-start.15

commit v2 on v1

--- a/solution.py
+++ b/solution.py
@@ -15,6 +15,7 @@
 
 CX, CY, NZ = 8, 48, 256
 NGX, NGY = 64, 8
+RX = 4
 MB = 32
 DB = 64
 SL = 64
@@ -38,12 +39,16 @@
 
 
 def kernel(
-    vel_h, pre_h, vis_h, wind, area, cell_s, cell_v, panels, shapes_t, nodes_t,
-    dnode, dvisc, dhyst, freq, ratio, modal, dstate,
-    vel_o, pre_o, modal_o, damp_o,
-    f0, f1, vis, xs, xr, ys, yr, samp, onehot, lhs, g0, h1, g2, h3,
-    in_sem, xss, xrs, yss, yrs, s_sem, r_sem,
+    vel_h, pre_h, vis_h, *refs,
 ):
+    small_h = refs[:14]
+    (
+        vel_o, pre_o, modal_o, damp_o,
+        wind, area, cell_s, cell_v, panels, shapes_t, nodes_t,
+        dnode, dvisc, dhyst, freq, ratio, modal, dstate,
+        f0, f1, vis, xs, xr, ys, yr, samp, onehot, lhs, g0, h1, g2, h3,
+        in_sem, small_sem, xss, xrs, yss, yrs, s_sem, r_sem, known,
+    ) = refs[14:]
     gx = lax.axis_index("gx")
     gy = lax.axis_index("gy")
     f32, bf16 = jnp.float32, jnp.bfloat16
@@ -56,22 +61,44 @@
 
     barrier = pltpu.get_barrier_semaphore()
 
-    def greet_gx(k, carry):
-        pl.semaphore_signal(barrier, 1, device_id=gx_peer(k))
-        return carry
-
-    def greet_gy(k, carry):
-        pl.semaphore_signal(barrier, 1, device_id=gy_peer(k))
-        return carry
-
-    lax.fori_loop(1, NGX, greet_gx, 0)
-    lax.fori_loop(1, NGY, greet_gy, 0)
+    plane, ring = gx // RX, lax.rem(gx, RX)
+
+    def z_peer(k):
+        return {"gx": lax.rem(plane + k, NGX // RX) * RX + ring}
+
+    def x_peer(k):
+        return {"gx": plane * RX + lax.rem(ring + k, RX)}
+
+    nz = NGX // RX
+    near = [gx_peer(1), gx_peer(NGX - 1)]
+    near += [z_peer(k) for k in (1, nz - 1, 2, nz - 2)]
+    near += [x_peer(k) for k in range(1, RX)]
+    near += [gy_peer(k) for k in range(1, NGY)]
+    for peer in near:
+        pl.semaphore_signal(barrier, 1, device_id=peer)
+
+    def tell(i, peers):
+        for peer in peers:
+            pl.semaphore_signal(known.at[i], 1, device_id=peer)
+
     cv = pltpu.make_async_copy(vel_h, f0.at[0:3, 1 : 1 + CX, Y0 : Y0 + CY, :], in_sem.at[0])
     cp = pltpu.make_async_copy(pre_h, f0.at[3, 1 : 1 + CX, Y0 : Y0 + CY, :], in_sem.at[1])
     cn = pltpu.make_async_copy(vis_h, vis, in_sem.at[2])
     cv.start()
     cp.start()
     cn.start()
+    small = [
+        pltpu.make_async_copy(src, dst, small_sem.at[i])
+        for i, (src, dst) in enumerate(
+            zip(
+                small_h,
+                (wind, area, cell_s, cell_v, panels, shapes_t, nodes_t,
+                 dnode, dvisc, dhyst, freq, ratio, modal, dstate),
+            )
+        )
+    ]
+    for c in small:
+        c.start()
     cv.wait()
     cp.wait()
 
@@ -119,12 +146,15 @@
 
     pack_x(f0, 0, range(4))
     pack_y(f0, 0, range(4))
-    pl.semaphore_wait(barrier, NGX - 1 + NGY - 1)
+    pl.semaphore_wait(barrier, len(near))
+    tell(0, [z_peer(2), z_peer(nz - 2)])
     hx1 = [x_copy(0, 0, d, 0, 4) for d in range(2)]
     hy1 = [y_copy(0, 0, d, 0, 4) for d in range(2)]
     for c in hy1 + hx1:
         c.start()
 
+    for c in small:
+        c.wait()
     dn = dnode[...]
     dn2 = jnp.concatenate([dn, dn], axis=1)
     node_no = lax.broadcasted_iota(jnp.int32, (nodes_t.shape[1], 2 * DB), 0)
@@ -207,6 +237,8 @@
         return carry
 
     cn.wait()
+    pl.semaphore_wait(known.at[0], 2)
+    tell(1, [z_peer(4), z_peer(nz - 4)])
     for c in hy1:
         c.wait_recv()
     unpack_y(f0, 0, range(4))
@@ -229,6 +261,8 @@
     hy3 = [y_copy(1, 1, d, 1, 4) for d in range(2)]
     for c in hx3 + hy3:
         c.start()
+    pl.semaphore_wait(known.at[1], 2)
+    tell(2, [x_peer(k) for k in range(1, RX)])
     for c in hx2 + hy2:
         c.wait_recv()
     unpack_x(f1, 1, (0,))
@@ -275,6 +309,7 @@
             most, most, s_sem.at[sem_no], r_sem.at[sem_no], device_id=gy_peer(1)
         )
 
+    pl.semaphore_wait(known.at[2], RX - 1)
     stage0 = all_gx(g0, 0)
     for c in hx3 + hy3:
         c.wait_recv()
@@ -349,27 +384,47 @@
     stage3.wait_send()
 
 
+def write_out(*refs):
+    n = len(refs) // 2
+    sem = refs[-1]
+    copies = [pltpu.make_async_copy(refs[i], refs[n + i], sem.at[i]) for i in range(n)]
+    for c in copies:
+        c.start()
+    for c in copies:
+        c.wait()
+
+
 def body(
     velocity, pressure, viscosity, wind_profile, panel_area, slot_cell, slot_panel, panel_shapes,
     node_shapes, damper_node, damper_viscous, damper_hysteretic, frequency, damping_ratio,
     modal_state, damper_state,
 ):
-    any_space = pl.BlockSpec(memory_space=pl.ANY)
+    hbm = pl.BlockSpec(memory_space=pltpu.MemorySpace.HBM)
     vmem = pl.BlockSpec(memory_space=pltpu.VMEM)
-    smem = pl.BlockSpec(memory_space=pltpu.SMEM)
     f32, bf16 = jnp.float32, jnp.bfloat16
     slots = slot_panel.shape[1]
-    vel, pre, modal, damp = pl.pallas_call(
+    small = (
+        wind_profile.reshape(1, -1), panel_area.reshape(1, -1),
+        slot_cell, slot_cell, slot_panel.reshape(slots // 128, 128), panel_shapes.T, node_shapes.T,
+        damper_node.reshape(1, -1), damper_viscous.reshape(1, -1), damper_hysteretic.reshape(1, -1),
+        frequency.reshape(1, -1), damping_ratio.reshape(1, -1), modal_state,
+        damper_state.reshape(1, -1),
+    )
+    outs = (
+        jax.ShapeDtypeStruct(velocity.shape, f32),
+        jax.ShapeDtypeStruct(pressure.shape, f32),
+        jax.ShapeDtypeStruct(modal_state.shape, f32),
+        jax.ShapeDtypeStruct((1, DB), f32),
+    )
+    held = [
+        (pltpu.SMEM if i == 2 else pltpu.VMEM)(a.shape, a.dtype) for i, a in enumerate(small)
+    ]
+    results = pl.pallas_call(
         kernel,
-        out_shape=(
-            jax.ShapeDtypeStruct(velocity.shape, f32),
-            jax.ShapeDtypeStruct(pressure.shape, f32),
-            jax.ShapeDtypeStruct(modal_state.shape, f32),
-            jax.ShapeDtypeStruct((1, DB), f32),
-        ),
-        in_specs=[any_space] * 3 + [vmem] * 2 + [smem] + [vmem] * 11,
+        out_shape=outs,
+        in_specs=[hbm] * (3 + len(small)),
         out_specs=(vmem,) * 4,
-        scratch_shapes=[
+        scratch_shapes=held + [
             pltpu.VMEM((4, CX + 2, CY + 16, NZ), f32),
             pltpu.VMEM((4, CX + 2, CY + 16, NZ), f32),
             pltpu.VMEM((CX, CY, NZ), f32),
@@ -385,23 +440,26 @@
             pltpu.VMEM((NGX, 1, 128), f32),
             pltpu.VMEM((NGY, 1, 128), f32),
             pltpu.SemaphoreType.DMA((3,)),
+            pltpu.SemaphoreType.DMA((len(small),)),
             pltpu.SemaphoreType.DMA((2, 4)),
             pltpu.SemaphoreType.DMA((2, 4)),
             pltpu.SemaphoreType.DMA((2, 4)),
             pltpu.SemaphoreType.DMA((2, 4)),
             pltpu.SemaphoreType.DMA((4,)),
             pltpu.SemaphoreType.DMA((4,)),
+            pltpu.SemaphoreType.REGULAR((3,)),
         ],
         compiler_params=pltpu.CompilerParams(
             collective_id=0, has_side_effects=True, vmem_limit_bytes=40 << 20
         ),
-    )(
-        velocity, pressure, viscosity, wind_profile.reshape(1, -1), panel_area.reshape(1, -1),
-        slot_cell, slot_cell, slot_panel.reshape(slots // 128, 128), panel_shapes.T, node_shapes.T,
-        damper_node.reshape(1, -1), damper_viscous.reshape(1, -1), damper_hysteretic.reshape(1, -1),
-        frequency.reshape(1, -1), damping_ratio.reshape(1, -1), modal_state,
-        damper_state.reshape(1, -1),
-    )
+    )(*[pltpu.with_memory_space_constraint(a, pltpu.MemorySpace.HBM) for a in (velocity, pressure, viscosity, *small)])
+    vel, pre, modal, damp = pl.pallas_call(
+        write_out,
+        out_shape=outs,
+        in_specs=[vmem] * 4,
+        out_specs=(hbm,) * 4,
+        scratch_shapes=[pltpu.SemaphoreType.DMA((4,))], compiler_params=pltpu.CompilerParams(vmem_limit_bytes=1 << 20),
+    )(*results)
     return vel, pre, modal, damp.reshape(-1)
 
 

time: 73 us -> 53.6 us (0.73)
  local copies, waits for them, and re-layouts: 15.2 us -> 0 us
  Pallas kernels: 56.7 us -> 52.8 us
    unnamed x36 -> x0, local copies, waits for them, and re-layouts: 15.2 us -> none
    pallas_call x1 -> x2, Pallas kernels: 56.7 us -> 52.8 us  [the longest x1 51.6 us: body(): pl.pallas_call(kernel, out_shape=outs, in_specs=[hbm] * (3 + len(small)),...]
where the time goes in v2:
time: 53.6 us; the launch traced here: 53.4 us
  Pallas kernels  52.8 us (99%)
  between operations  0.65 us (1%)
    pallas_call x1, Pallas kernels, body(): pl.pallas_call(kernel, out_shape=outs, in_specs=[hbm] * (3 + len(small)),...  51.6 us
    pallas_call x1, Pallas kernels, body(): pl.pallas_call(write_out, out_shape=outs, in_specs=[vmem] * 4, out_specs=...  1.18 us

profile of v2, /device:TPU:1, one launch (start us, length us, event | category | flops | bytes accessed | tf_op | source)
XLA Modules:
  0.0 53.4 jit_solution(2280516829818485015)
XLA Ops:
  0.6 51.6 %shard_map.183 = (f32[3,8,48,256]{3,2,1,0:T(8,128)S(1)}, f32[8,48,256]{2,1,0:T(8,128)S(1)}, f32[2,32]{1,0:T(2,128)S(1)}, f32[1,64]{1,0:T(1,128)S(1)}) custom-call(f32[3,8,48,256]{3,2,1,0:T(8,128)} %vel_h.1, f32[8,48,256]{2,1,0:T(8,128)} %pre_h.1, f32[8,48,256]{2,1,0:T(8,128)} %vis_h.1, f32[1,256]{1,0:T(1,128)} %bitcast.16, f32[1,2048]{1,0:T(1,128)} %bitcast.15, ...), custom_call_target="tpu_custom_call" | custom-call | tf_op jit(solution)/shard_map/pallas_call | solution.py:422
  52.2 1.2 %shard_map.184 = (f32[3,8,48,256]{3,2,1,0:T(8,128)}, f32[8,48,256]{2,1,0:T(8,128)}, f32[2,32]{1,0:T(2,128)}, f32[1,64]{1,0:T(1,128)}) custom-call(f32[3,8,48,256]{3,2,1,0:T(8,128)S(1)} %get-tuple-element.12.refs_0_, f32[8,48,256]{2,1,0:T(8,128)S(1)} %get-tuple-element.13.refs_1_, f32[2,32]{1,0:T(2,128)S(1)} %get-tuple-element.14.refs_2_, ...), custom_call_target="tpu_custom_call" | custom-call | tf_op jit(solution)/shard_map/pallas_call | solution.py:456

commit v3 on v2

--- a/solution.py
+++ b/solution.py
@@ -38,6 +38,10 @@
     return jnp.sum(jnp.where(lane == sub + lane_shift, row, zero), axis=1, keepdims=True)
 
 
+def twice(row):
+    return jnp.concatenate([row, row], axis=1)
+
+
 def kernel(
     vel_h, pre_h, vis_h, *refs,
 ):
@@ -46,7 +50,8 @@
         vel_o, pre_o, modal_o, damp_o,
         wind, area, cell_s, cell_v, panels, shapes_t, nodes_t,
         dnode, dvisc, dhyst, freq, ratio, modal, dstate,
-        f0, f1, vis, xs, xr, ys, yr, samp, onehot, lhs, g0, h1, g2, h3,
+        f0, f1, vis, xs, xr, ys, yr, samp, onehot, lhs,
+        shapes_x, nodes_x, pick_all, drift_x, ring_b, dampers_b, g0, h1, g2, late,
         in_sem, small_sem, xss, xrs, yss, yrs, s_sem, r_sem, known,
     ) = refs[14:]
     gx = lax.axis_index("gx")
@@ -74,6 +79,7 @@
     near += [z_peer(k) for k in (1, nz - 1, 2, nz - 2)]
     near += [x_peer(k) for k in range(1, RX)]
     near += [gy_peer(k) for k in range(1, NGY)]
+    ring_peers = [x_peer(k) for k in range(1, RX)]
     for peer in near:
         pl.semaphore_signal(barrier, 1, device_id=peer)
 
@@ -147,7 +153,7 @@
     pack_x(f0, 0, range(4))
     pack_y(f0, 0, range(4))
     pl.semaphore_wait(barrier, len(near))
-    tell(0, [z_peer(2), z_peer(nz - 2)])
+    tell(0, [z_peer(2), z_peer(nz - 2)] + ring_peers)
     hx1 = [x_copy(0, 0, d, 0, 4) for d in range(2)]
     hy1 = [y_copy(0, 0, d, 0, 4) for d in range(2)]
     for c in hy1 + hx1:
@@ -155,29 +161,59 @@
 
     for c in small:
         c.wait()
-    dn = dnode[...]
-    dn2 = jnp.concatenate([dn, dn], axis=1)
-    node_no = lax.broadcasted_iota(jnp.int32, (nodes_t.shape[1], 2 * DB), 0)
-    pick = jnp.where(node_no == dn2 + 1, 1.0, jnp.where(node_no == dn2, -1.0, 0.0)).astype(bf16)
-    drift = jnp.dot(nodes_t[...], pick, preferred_element_type=f32)
+    dn = dnode[...].astype(f32)
+    dn2 = twice(dn)
+    node_no = lax.broadcasted_iota(jnp.int32, (nodes_t.shape[1], 2 * DB), 0).astype(f32)
+
+    def pick(row):
+        return jnp.where(node_no == row + 1.0, 1.0, jnp.where(node_no == row, -1.0, 0.0)).astype(bf16)
+
+    drift = jnp.dot(nodes_t[...], pick(dn2), preferred_element_type=f32)
     q0 = column_of(modal[0:1, :], MB)
     v0 = column_of(modal[1:2, :], MB)
-    omega = column_of(freq[...], MB)
-    zeta = column_of(ratio[...], MB)
     first_half = lax.broadcasted_iota(jnp.int32, (MB, 2 * DB), 1) < DB
-
-    def stretch_row(q, v):
-        return jnp.sum(drift * jnp.where(first_half, q, v), axis=0, keepdims=True)
-
-    g0[gx, 1:2, :] = stretch_row(q0, v0)
+    odd = lax.rem(gy, 2)
+    own_half = (lax.broadcasted_iota(jnp.int32, (1, 2 * DB), 1) // DB) == odd
+
+    def placed_half(row):
+        return jnp.where(own_half, twice(row), 0.0)
+
+    dampers_b[gy, 0:1, :] = placed_half(dvisc[...])
+    dampers_b[gy, 1:2, :] = placed_half(dhyst[...])
+    dampers_b[gy, 2:3, :] = placed_half(dn)
+    ring_b[ring, 0:1, :] = jnp.sum(
+        drift * jnp.where(first_half, q0, v0), axis=0, keepdims=True
+    )
+    ring_b[ring, 1:2, :] = row_of(q0, MB * ring)
+    ring_b[ring, 2:3, :] = row_of(v0, MB * ring)
+    ring_b[ring, 3:4, :] = row_of(column_of(freq[...], MB), MB * ring)
+    ring_b[ring, 4:5, :] = row_of(column_of(ratio[...], MB), MB * ring)
+
+    def spread(buf, me, count, sem_no, peer):
+        def send(k, carry):
+            pltpu.make_async_remote_copy(
+                buf.at[me], buf.at[me], s_sem.at[sem_no], r_sem.at[sem_no], device_id=peer(k)
+            ).start()
+            return carry
+
+        lax.fori_loop(1, count, send, 0)
+        most = buf.at[pl.ds(0, count - 1)]
+        return pltpu.make_async_remote_copy(
+            most, most, s_sem.at[sem_no], r_sem.at[sem_no], device_id=peer(1)
+        )
+
+    ring_stage = spread(ring_b, ring, RX, 0, x_peer)
+    damper_stage = spread(dampers_b, gy, NGY, 1, gy_peer)
 
     def table(i, carry):
-        low = panels[pl.ds(i, 1), :] & 127
+        low = panels[pl.ds(2 * i + ring // 2, 1), :] & 127
         sub = lax.broadcasted_iota(jnp.int32, (128, 128), 0)
         onehot[:, pl.ds(pl.multiple_of(i * 128, 128), 128)] = (sub == low).astype(f32).astype(bf16)
         return carry
 
-    lax.fori_loop(0, panels.shape[0], table, 0)
+    lax.fori_loop(0, nz, table, 0)
+    shapes_x[ring] = shapes_t[...]
+    nodes_x[ring] = nodes_t[...]
     parity = lax.rem(gx, 2)
     own_ids = column_of(panels[pl.ds(gx // 2, 1), :], SL, SL * parity)
     panel_no = lax.broadcasted_iota(jnp.int32, (SL, area.shape[1]), 1)
@@ -237,7 +273,7 @@
         return carry
 
     cn.wait()
-    pl.semaphore_wait(known.at[0], 2)
+    pl.semaphore_wait(known.at[0], 2 + len(ring_peers))
     tell(1, [z_peer(4), z_peer(nz - 4)])
     for c in hy1:
         c.wait_recv()
@@ -255,14 +291,13 @@
     hy2 = [y_copy(1, 0, d, 0, 1) for d in range(2)]
     for c in hx2 + hy2:
         c.start()
+    shapes_stage = spread(shapes_x, ring, RX, 2, x_peer)
     pack_x(f1, 1, (1, 2, 3))
     pack_y(f1, 1, (1, 2, 3))
     hx3 = [x_copy(1, 1, d, 1, 4) for d in range(2)]
     hy3 = [y_copy(1, 1, d, 1, 4) for d in range(2)]
     for c in hx3 + hy3:
         c.start()
-    pl.semaphore_wait(known.at[1], 2)
-    tell(2, [x_peer(k) for k in range(1, RX)])
     for c in hx2 + hy2:
         c.wait_recv()
     unpack_x(f1, 1, (0,))
@@ -277,40 +312,16 @@
 
     for s in range(SL):
         line = cell_s[0, s] >> 8
-        plane = line // CY
-        samp[s : s + 1, :] = pre_o[plane, pl.ds(line - plane * CY, 1), :]
+        layer = line // CY
+        samp[s : s + 1, :] = pre_o[layer, pl.ds(line - layer * CY, 1), :]
     sampled = jnp.sum(jnp.where(z_mask, samp[...], 0.0), axis=1, keepdims=True)
     load = (own_area * sampled).astype(bf16).astype(f32)
-    g0[gx, 0:1, :] = row_of(load, SL * parity)
-
-    def all_gx(buf, sem_no):
-        def send(k, carry):
-            pltpu.make_async_remote_copy(
-                buf.at[gx], buf.at[gx], s_sem.at[sem_no], r_sem.at[sem_no], device_id=gx_peer(k)
-            ).start()
-            return carry
-
-        lax.fori_loop(1, NGX, send, 0)
-        most = buf.at[pl.ds(0, NGX - 1)]
-        return pltpu.make_async_remote_copy(
-            most, most, s_sem.at[sem_no], r_sem.at[sem_no], device_id=gx_peer(1)
-        )
-
-    def all_gy(buf, sem_no):
-        def send(k, carry):
-            pltpu.make_async_remote_copy(
-                buf.at[gy], buf.at[gy], s_sem.at[sem_no], r_sem.at[sem_no], device_id=gy_peer(k)
-            ).start()
-            return carry
-
-        lax.fori_loop(1, NGY, send, 0)
-        most = buf.at[pl.ds(0, NGY - 1)]
-        return pltpu.make_async_remote_copy(
-            most, most, s_sem.at[sem_no], r_sem.at[sem_no], device_id=gy_peer(1)
-        )
-
-    pl.semaphore_wait(known.at[2], RX - 1)
-    stage0 = all_gx(g0, 0)
+    g0[plane, 0:1, :] = row_of(load, SL * parity)
+    ring_stage.wait_recv()
+    g0[plane, 1:2, :] = jnp.sum(ring_b[:, 0:1, :], axis=0)
+    pl.semaphore_wait(known.at[1], 2)
+    stage0 = spread(g0, plane, nz, 3, z_peer)
+    nodes_stage = spread(nodes_x, ring, RX, 4, x_peer)
     for c in hx3 + hy3:
         c.wait_recv()
     unpack_x(f1, 1, (1, 2, 3))
@@ -324,41 +335,72 @@
         return carry
 
     lax.fori_loop(1, CX + 1, second_velocity, 0)
-    for c in hx1 + hy1 + hx2 + hy2 + hx3 + hy3:
+    for c in hx1 + hy1 + hx2 + hy2 + hx3 + hy3 + [ring_stage, damper_stage]:
         c.wait_send()
-
+    damper_stage.wait_recv()
+
+    def paired(buf, row):
+        return jnp.concatenate(
+            [buf[2 * j, row : row + 1, :] + buf[2 * j + 1, row : row + 1, :] for j in range(NGY // 2)],
+            axis=0,
+        )
+
+    visc_all, hyst_all, node_all = (paired(dampers_b, r) for r in range(3))
+    for j in range(NGY // 2):
+        pick_all[:, j * 128 : (j + 1) * 128] = pick(node_all[j : j + 1, :])
+    q0_row, v0_row, omega, zeta = (jnp.sum(ring_b[:, r : r + 1, :], axis=0) for r in range(1, 5))
+
+    shapes_stage.wait_recv()
     stage0.wait_recv()
     sub16 = lax.broadcasted_iota(jnp.int32, (16, 128), 0)
-    for i in range(NGX // 2):
-        pair = g0[2 * i, 0:1, :] + g0[2 * i + 1, 0:1, :]
-        high = panels[i : i + 1, :] >> 7
-        lhs[:, i * 128 : (i + 1) * 128] = jnp.where(sub16 == high, pair, 0.0).astype(bf16)
+    for i in range(nz):
+        high = panels[pl.ds(2 * i + ring // 2, 1), :] >> 7
+        lhs[:, i * 128 : (i + 1) * 128] = jnp.where(sub16 == high, g0[i, 0:1, :], 0.0).astype(bf16)
     placed = lax.dot_general(
         lhs[...], onehot[...], (((1,), (1,)), ((), ())), preferred_element_type=f32
     )
-    part = jnp.zeros((MB, 128), f32)
-    for a in range(16):
-        part = part + shapes_t[:, a * 128 : (a + 1) * 128].astype(f32) * placed[a : a + 1, :]
-    panel_part = jnp.sum(part, axis=1, keepdims=True)
-
-    def response(total, hysteresis):
-        stretch = total[:, 0:DB]
-        rate = total[:, DB : 2 * DB]
+    parts = []
+    for r in range(RX):
+        part = jnp.zeros((MB, 128), f32)
+        for a in range(16):
+            part = part + shapes_x[r, :, a * 128 : (a + 1) * 128].astype(f32) * placed[a : a + 1, :]
+        parts.append(row_of(jnp.sum(part, axis=1, keepdims=True), MB * r))
+
+    def response(stretch, rate, viscous, hysteretic, hysteresis):
         hysteresis = hysteresis + modal_step * (
             hysteresis_gain * rate
             - shape_beta * jnp.abs(rate) * hysteresis
             - shape_gamma * rate * jnp.abs(hysteresis)
         )
-        force = -(dvisc[...] * rate + spring_rate * stretch + dhyst[...] * hysteresis)
-        return hysteresis, jnp.sum(drift[:, 0:DB] * force, axis=1, keepdims=True)
-
-    hysteresis, damper_part = response(jnp.sum(g0[:, 1:2, :], axis=0), dstate[...])
-    h1[gy] = row_of(panel_part) + row_of(damper_part, MB)
-    stage1 = all_gy(h1, 1)
+        return hysteresis, -(viscous * rate + spring_rate * stretch + hysteretic * hysteresis)
+
+    first = jnp.sum(g0[:, 1:2, :], axis=0)
+    stretch0 = first[:, 0:DB]
+    hysteresis, force = response(stretch0, first[:, DB : 2 * DB], dvisc[...], dhyst[...], dstate[...])
+    damper_part = jnp.sum(drift[:, 0:DB] * force, axis=1, keepdims=True)
+    spot = ring * NGY + gy
+    h1[spot, 0:1, :] = (parts[0] + parts[1]) + (parts[2] + parts[3])
+    h1[spot, 1:2, :] = row_of(damper_part, MB * ring)
+    h1[spot, 2:3, :] = placed_half(stretch0)
+    h1[spot, 3:4, :] = placed_half(hysteresis)
+
+    def plane_peer(k):
+        there = lax.rem(spot + k, RX * NGY)
+        return {"gx": plane * RX + there // NGY, "gy": lax.rem(there, NGY)}
+
+    stage1 = spread(h1, spot, RX * NGY, 5, plane_peer)
     stage0.wait_send()
+    shapes_stage.wait_send()
+    nodes_stage.wait_recv()
+    for r in range(RX):
+        drift_x[r * MB : (r + 1) * MB, :] = jnp.dot(
+            nodes_x[r], pick_all[...], preferred_element_type=f32
+        )
+    nodes_stage.wait_send()
     stage1.wait_recv()
-    total1 = jnp.sum(h1[...], axis=0)
-    panel_modal = column_of(total1, MB)
+    panel_modal = jnp.sum(h1[:, 0:1, :], axis=0)
+    damper_modal = jnp.sum(h1[:, 1:2, :], axis=0)
+    stretch_all, hysteresis_all = paired(h1, 2), paired(h1, 3)
 
     def advance_modes(q, v, damper_load):
         acceleration = (
@@ -367,21 +409,30 @@
         v = v + modal_step * acceleration
         return q + modal_step * v, v
 
-    q1, v1 = advance_modes(q0, v0, column_of(total1, MB, MB))
-    g2[gx] = stretch_row(q1, v1)
-    stage2 = all_gx(g2, 2)
+    q1, v1 = advance_modes(q0_row, v0_row, damper_modal)
+    v1_column = column_of(v1, RX * MB)
+    for j in range(NGY // 2):
+        g2[plane, j : j + 1, :] = jnp.sum(
+            drift_x[:, j * 128 : (j + 1) * 128] * v1_column, axis=0, keepdims=True
+        )
+    stage2 = spread(g2, plane, nz, 6, z_peer)
     stage1.wait_send()
     stage2.wait_recv()
-    hysteresis, damper_part = response(jnp.sum(g2[...], axis=0), hysteresis)
-    damp_o[...] = hysteresis
-    h3[gy] = row_of(damper_part)
-    stage3 = all_gy(h3, 3)
+    rate_all = jnp.sum(g2[...], axis=0)
+    stretch_all = stretch_all + modal_step * rate_all
+    hysteresis_all, force = response(stretch_all, rate_all, visc_all, hyst_all, hysteresis_all)
+    late[...] = hysteresis_all
+    own = late[pl.ds(gy // 2, 1), :]
+    damp_o[...] = jnp.where(odd == 1, own[:, DB : 2 * DB], own[:, 0:DB])
+    part = jnp.zeros((MB, 128), f32)
+    for j in range(NGY // 2):
+        rows = pl.ds(pl.multiple_of(ring * MB, MB), MB)
+        part = part + drift_x[rows, j * 128 : (j + 1) * 128] * force[j : j + 1, :]
+    damper_modal = row_of(jnp.sum(part, axis=1, keepdims=True), MB * ring)
+    q2, v2 = advance_modes(q1, v1, damper_modal)
+    modal_o[0:1, :] = row_of(column_of(q2, MB, MB * ring), 0, MB)
+    modal_o[1:2, :] = row_of(column_of(v2, MB, MB * ring), 0, MB)
     stage2.wait_send()
-    stage3.wait_recv()
-    q2, v2 = advance_modes(q1, v1, column_of(jnp.sum(h3[...], axis=0), MB))
-    modal_o[0:1, :] = row_of(q2, 0, MB)
-    modal_o[1:2, :] = row_of(v2, 0, MB)
-    stage3.wait_send()
 
 
 def write_out(*refs):
@@ -433,21 +484,27 @@
             pltpu.VMEM((2, 2, 4, CX, NZ), f32),
             pltpu.VMEM((2, 2, 4, CX, NZ), f32),
             pltpu.VMEM((SL, NZ), f32),
-            pltpu.VMEM((128, slots), bf16),
-            pltpu.VMEM((16, slots), bf16),
-            pltpu.VMEM((NGX, 2, 128), f32),
-            pltpu.VMEM((NGY, 1, 128), f32),
-            pltpu.VMEM((NGX, 1, 128), f32),
-            pltpu.VMEM((NGY, 1, 128), f32),
+            pltpu.VMEM((128, NGX // RX * 128), bf16),
+            pltpu.VMEM((16, NGX // RX * 128), bf16),
+            pltpu.VMEM((RX,) + panel_shapes.shape[::-1], bf16),
+            pltpu.VMEM((RX,) + node_shapes.shape[::-1], bf16),
+            pltpu.VMEM((node_shapes.shape[0], DB * NGY), bf16),
+            pltpu.VMEM((RX * MB, DB * NGY), f32),
+            pltpu.VMEM((RX, 8, 128), f32),
+            pltpu.VMEM((NGY, 4, 128), f32),
+            pltpu.VMEM((NGX // RX, 2, 128), f32),
+            pltpu.VMEM((RX * NGY, 4, 128), f32),
+            pltpu.VMEM((NGX // RX, NGY // 2, 128), f32),
+            pltpu.VMEM((NGY // 2, 128), f32),
             pltpu.SemaphoreType.DMA((3,)),
             pltpu.SemaphoreType.DMA((len(small),)),
             pltpu.SemaphoreType.DMA((2, 4)),
             pltpu.SemaphoreType.DMA((2, 4)),
             pltpu.SemaphoreType.DMA((2, 4)),
             pltpu.SemaphoreType.DMA((2, 4)),
-            pltpu.SemaphoreType.DMA((4,)),
-            pltpu.SemaphoreType.DMA((4,)),
-            pltpu.SemaphoreType.REGULAR((3,)),
+            pltpu.SemaphoreType.DMA((7,)),
+            pltpu.SemaphoreType.DMA((7,)),
+            pltpu.SemaphoreType.REGULAR((2,)),
         ],
         compiler_params=pltpu.CompilerParams(
             collective_id=0, has_side_effects=True, vmem_limit_bytes=40 << 20

time: 53.6 us -> 47.7 us (0.89)
  Pallas kernels: 52.8 us -> 46.9 us
    pallas_call x1, Pallas kernels: 51.6 us -> 45.7 us  [body(): pl.pallas_call(kernel, out_shape=outs, in_specs=[hbm] * (3 + len(small)),...]
where the time goes in v3:
time: 47.7 us; the launch traced here: 47.6 us
  Pallas kernels  46.9 us (98%)
  between operations  0.65 us (1%)
    pallas_call x1, Pallas kernels, body(): pl.pallas_call(kernel, out_shape=outs, in_specs=[hbm] * (3 + len(small)),...  45.7 us
    pallas_call x1, Pallas kernels, body(): pl.pallas_call(write_out, out_shape=outs, in_specs=[vmem] * 4, out_specs=...  1.18 us

profile of v3, /device:TPU:1, one launch (start us, length us, event | category | flops | bytes accessed | tf_op | source)
XLA Modules:
  0.0 47.6 jit_solution(85909737763121648)
XLA Ops:
  0.6 45.7 %shard_map.183 = (f32[3,8,48,256]{3,2,1,0:T(8,128)S(1)}, f32[8,48,256]{2,1,0:T(8,128)S(1)}, f32[2,32]{1,0:T(2,128)S(1)}, f32[1,64]{1,0:T(1,128)S(1)}) custom-call(f32[3,8,48,256]{3,2,1,0:T(8,128)} %vel_h.1, f32[8,48,256]{2,1,0:T(8,128)} %pre_h.1, f32[8,48,256]{2,1,0:T(8,128)} %vis_h.1, f32[1,256]{1,0:T(1,128)} %bitcast.16, f32[1,2048]{1,0:T(1,128)} %bitcast.15, ...), custom_call_target="tpu_custom_call" | custom-call | tf_op jit(solution)/shard_map/pallas_call | solution.py:473
  46.4 1.2 %shard_map.184 = (f32[3,8,48,256]{3,2,1,0:T(8,128)}, f32[8,48,256]{2,1,0:T(8,128)}, f32[2,32]{1,0:T(2,128)}, f32[1,64]{1,0:T(1,128)}) custom-call(f32[3,8,48,256]{3,2,1,0:T(8,128)S(1)} %get-tuple-element.12.refs_0_, f32[8,48,256]{2,1,0:T(8,128)S(1)} %get-tuple-element.13.refs_1_, f32[2,32]{1,0:T(2,128)S(1)} %get-tuple-element.14.refs_2_, ...), custom_call_target="tpu_custom_call" | custom-call | tf_op jit(solution)/shard_map/pallas_call | solution.py:513

commit v4 on v3

--- a/solution.py
+++ b/solution.py
@@ -50,9 +50,9 @@
         vel_o, pre_o, modal_o, damp_o,
         wind, area, cell_s, cell_v, panels, shapes_t, nodes_t,
         dnode, dvisc, dhyst, freq, ratio, modal, dstate,
-        f0, f1, vis, xs, xr, ys, yr, samp, onehot, lhs,
+        f0, f1, vis, xs, xr, ys, yr, yi, cs, cr, samp, onehot, lhs,
         shapes_x, nodes_x, pick_all, drift_x, ring_b, dampers_b, g0, h1, g2, late,
-        in_sem, small_sem, xss, xrs, yss, yrs, s_sem, r_sem, known,
+        in_sem, small_sem, xss, xrs, yss, yrs, css, crs, s_sem, r_sem, known,
     ) = refs[14:]
     gx = lax.axis_index("gx")
     gy = lax.axis_index("gy")
@@ -150,16 +150,72 @@
                     gy == NGY - 1, 0.0, yr[p, 1, q, x : x + 1, :]
                 )
 
+    lane8 = lax.broadcasted_iota(jnp.int32, (8, NZ), 1)
+
+    def above(v):
+        return jnp.where(lane8 == NZ - 1, 0.0, pltpu.roll(v, NZ - 1, 1))
+
+    def below(v):
+        return jnp.where(lane8 == 0, 0.0, pltpu.roll(v, 1, 1))
+
+    small[0].wait()
+    w_row = jnp.broadcast_to((-0.5 * time_step) * wind[...], (8, NZ))
+    half = 0.5 * time_step
+
+    x8 = lax.broadcasted_iota(jnp.int32, (CX, NZ), 0)
+
+    def next_x(v):
+        return jnp.where(x8 == CX - 1, 0.0, pltpu.roll(v, CX - 1, 0))
+
+    def last_x(v):
+        return jnp.where(x8 == 0, 0.0, pltpu.roll(v, 1, 0))
+
+    def outer_x(d):
+        x, inner, sign = (CX, CX - 1, 1.0) if d == 0 else (1, 2, -1.0)
+        zero = jnp.zeros((1, NZ), f32)
+        f0[0, x, Y0 - 1 : Y0, :] = zero
+        f0[0, x, Y0 + CY : Y0 + CY + 1, :] = zero
+        for t in range(YT):
+            rows = pl.ds(Y0 + 8 * t, 8)
+            own = slice(8 * t, 8 * t + 8)
+            c, i, p = f0[0, x, rows, :], f0[0, inner, rows, :], f0[3, inner, rows, :]
+            r, l = f0[0, x, pl.ds(Y0 + 8 * t + 1, 8), :], f0[0, x, pl.ds(Y0 + 8 * t - 1, 8), :]
+            lap = (i + (r + l)) + ((above(c) + below(c)) - 6.0 * c)
+            nu = time_step * vis[x - 1, own, :]
+            tile = c + (nu * lap + sign * (half * p - w_row * i))
+            yield own, tile, vis[x - 1, own, :]
+
+    def pack_outer_x():
+        for d in range(2):
+            for own, tile, nu in outer_x(d):
+                xs[0, d, 4, own, :] = tile.astype(bf16)
+                xs[0, d, 5, own, :] = nu.astype(bf16)
+
+    def pack_outer_y():
+        for d in range(2):
+            y, inner, sign = (Y0 + CY - 1, Y0 + CY - 2, 1.0) if d == 0 else (Y0, Y0 + 1, -1.0)
+            for x in range(CX):
+                yi[d, 0, x : x + 1, :] = f0[1, x + 1, inner : inner + 1, :]
+                yi[d, 1, x : x + 1, :] = f0[3, x + 1, inner : inner + 1, :]
+                ys[0, d, 5, x : x + 1, :] = vis[x, y - Y0 : y - Y0 + 1, :]
+            c, nu = ys[0, d, 0], time_step * ys[0, d, 5]
+            a, b = next_x(c), last_x(c)
+            lap = (yi[d, 0] + (a + b)) + ((above(c) + below(c)) - 6.0 * c)
+            ys[0, d, 4] = c + (w_row * (a - b) + nu * lap + (sign * half) * yi[d, 1])
+
+    pack_y(f0, 0, range(4))
+    cn.wait()
+    pack_outer_y()
     pack_x(f0, 0, range(4))
-    pack_y(f0, 0, range(4))
+    pack_outer_x()
     pl.semaphore_wait(barrier, len(near))
     tell(0, [z_peer(2), z_peer(nz - 2)] + ring_peers)
-    hx1 = [x_copy(0, 0, d, 0, 4) for d in range(2)]
-    hy1 = [y_copy(0, 0, d, 0, 4) for d in range(2)]
+    hx1 = [x_copy(0, 0, d, 0, 6) for d in range(2)]
+    hy1 = [y_copy(0, 0, d, 0, 6) for d in range(2)]
     for c in hy1 + hx1:
         c.start()
 
-    for c in small:
+    for c in small[1:]:
         c.wait()
     dn = dnode[...].astype(f32)
     dn2 = twice(dn)
@@ -205,32 +261,12 @@
     ring_stage = spread(ring_b, ring, RX, 0, x_peer)
     damper_stage = spread(dampers_b, gy, NGY, 1, gy_peer)
 
-    def table(i, carry):
-        low = panels[pl.ds(2 * i + ring // 2, 1), :] & 127
-        sub = lax.broadcasted_iota(jnp.int32, (128, 128), 0)
-        onehot[:, pl.ds(pl.multiple_of(i * 128, 128), 128)] = (sub == low).astype(f32).astype(bf16)
-        return carry
-
-    lax.fori_loop(0, nz, table, 0)
-    shapes_x[ring] = shapes_t[...]
-    nodes_x[ring] = nodes_t[...]
     parity = lax.rem(gx, 2)
     own_ids = column_of(panels[pl.ds(gx // 2, 1), :], SL, SL * parity)
     panel_no = lax.broadcasted_iota(jnp.int32, (SL, area.shape[1]), 1)
     own_area = jnp.sum(jnp.where(panel_no == own_ids, area[...], 0.0), axis=1, keepdims=True)
     own_z = column_of(cell_v[...], SL) & (NZ - 1)
     z_mask = (lax.broadcasted_iota(jnp.int32, (SL, NZ), 1) == own_z)
-
-    lane8 = lax.broadcasted_iota(jnp.int32, (8, NZ), 1)
-
-    def above(v):
-        return jnp.where(lane8 == NZ - 1, 0.0, pltpu.roll(v, NZ - 1, 1))
-
-    def below(v):
-        return jnp.where(lane8 == 0, 0.0, pltpu.roll(v, 1, 1))
-
-    w_row = jnp.broadcast_to((-0.5 * time_step) * wind[...], (8, NZ))
-    half = 0.5 * time_step
 
     def velocity_tile(f, x, t):
         rows = pl.ds(Y0 + 8 * t, 8)
@@ -272,12 +308,25 @@
             f1[3, x, rows, :] = pressure_tile(f0, x, t)
         return carry
 
-    cn.wait()
+    for c in hy1:
+        c.wait_recv()
+    corners = []
+    for d in range(2):
+        x = CX - 1 if d == 0 else 0
+        for side in range(2):
+            for q in range(2):
+                i = 2 * side + q
+                cs[d, i : i + 1, :] = yr[0, side, q, x : x + 1, :]
+        corners.append(
+            pltpu.make_async_remote_copy(
+                cs.at[d], cr.at[d], css.at[d], crs.at[d],
+                device_id=gx_peer(1 if d == 0 else NGX - 1),
+            )
+        )
+        corners[d].start()
+    unpack_y(f0, 0, range(4))
     pl.semaphore_wait(known.at[0], 2 + len(ring_peers))
     tell(1, [z_peer(4), z_peer(nz - 4)])
-    for c in hy1:
-        c.wait_recv()
-    unpack_y(f0, 0, range(4))
     lax.fori_loop(2, CX, first_layer, 0)
     for c in hx1:
         c.wait_recv()
@@ -285,23 +334,46 @@
     first_layer(1, 0)
     first_layer(CX, 0)
 
-    pack_x(f1, 1, (0,))
-    pack_y(f1, 1, (0,))
-    hx2 = [x_copy(1, 0, d, 0, 1) for d in range(2)]
-    hy2 = [y_copy(1, 0, d, 0, 1) for d in range(2)]
-    for c in hx2 + hy2:
-        c.start()
-    shapes_stage = spread(shapes_x, ring, RX, 2, x_peer)
     pack_x(f1, 1, (1, 2, 3))
     pack_y(f1, 1, (1, 2, 3))
     hx3 = [x_copy(1, 1, d, 1, 4) for d in range(2)]
     hy3 = [y_copy(1, 1, d, 1, 4) for d in range(2)]
     for c in hx3 + hy3:
         c.start()
-    for c in hx2 + hy2:
+    shapes_x[ring] = shapes_t[...]
+    shapes_stage = spread(shapes_x, ring, RX, 2, x_peer)
+
+    for c in corners:
         c.wait_recv()
-    unpack_x(f1, 1, (0,))
-    unpack_y(f1, 1, (0,))
+    for d in range(2):
+        x, far, sign = (1, 0, 1.0) if d == 0 else (CX, CX + 1, -1.0)
+        edge = gx == (0 if d == 0 else NGX - 1)
+        for t in range(YT):
+            rows, own = slice(Y0 + 8 * t, Y0 + 8 * t + 8), slice(8 * t, 8 * t + 8)
+            u, p = f0[0, x, rows, :], f0[3, x, rows, :]
+            nu = time_step * xr[0, d, 5, own, :].astype(f32)
+            tile = xr[0, d, 4, own, :].astype(f32) + (nu * u + sign * (w_row * u - half * p))
+            if t == 0:
+                corner = jnp.where(gy == 0, 0.0, cr[d, 1:2, :])
+                tile = tile + jnp.where(x8 == 0, nu * corner, 0.0)
+            if t == YT - 1:
+                corner = jnp.where(gy == NGY - 1, 0.0, cr[d, 3:4, :])
+                tile = tile + jnp.where(x8 == 7, nu * corner, 0.0)
+            f1[0, far, rows, :] = jnp.where(edge, 0.0, tile)
+    for d in range(2):
+        sign = 1.0 if d == 0 else -1.0
+        edge = gy == (0 if d == 0 else NGY - 1)
+        u, p = ys[0, 1 - d, 0], ys[0, 1 - d, 3]
+        nu = time_step * yr[0, d, 5]
+        low = jnp.where(gx == 0, 0.0, cr[0, 2 * d : 2 * d + 1, :])
+        high = jnp.where(gx == NGX - 1, 0.0, cr[1, 2 * d : 2 * d + 1, :])
+        tile = yr[0, d, 4] + (nu * u - (sign * half) * p)
+        tile = tile + jnp.where(x8 == 0, (nu - w_row) * low, 0.0)
+        tile = tile + jnp.where(x8 == CX - 1, (nu + w_row) * high, 0.0)
+        yi[d, 0] = jnp.where(edge, 0.0, tile)
+        y = Y0 - 1 if d == 0 else Y0 + CY
+        for x in range(CX):
+            f1[1, x + 1, y : y + 1, :] = yi[d, 0, x : x + 1, :]
 
     def second_pressure(x, carry):
         for t in range(YT):
@@ -321,6 +393,7 @@
     g0[plane, 1:2, :] = jnp.sum(ring_b[:, 0:1, :], axis=0)
     pl.semaphore_wait(known.at[1], 2)
     stage0 = spread(g0, plane, nz, 3, z_peer)
+    nodes_x[ring] = nodes_t[...]
     nodes_stage = spread(nodes_x, ring, RX, 4, x_peer)
     for c in hx3 + hy3:
         c.wait_recv()
@@ -335,9 +408,17 @@
         return carry
 
     lax.fori_loop(1, CX + 1, second_velocity, 0)
-    for c in hx1 + hy1 + hx2 + hy2 + hx3 + hy3 + [ring_stage, damper_stage]:
+    for c in hx1 + hy1 + corners + hx3 + hy3 + [ring_stage, damper_stage]:
         c.wait_send()
     damper_stage.wait_recv()
+
+    def table(i, carry):
+        low = panels[pl.ds(2 * i + ring // 2, 1), :] & 127
+        sub = lax.broadcasted_iota(jnp.int32, (128, 128), 0)
+        onehot[:, pl.ds(pl.multiple_of(i * 128, 128), 128)] = (sub == low).astype(f32).astype(bf16)
+        return carry
+
+    lax.fori_loop(0, nz, table, 0)
 
     def paired(buf, row):
         return jnp.concatenate(
@@ -392,10 +473,9 @@
     stage0.wait_send()
     shapes_stage.wait_send()
     nodes_stage.wait_recv()
-    for r in range(RX):
-        drift_x[r * MB : (r + 1) * MB, :] = jnp.dot(
-            nodes_x[r], pick_all[...], preferred_element_type=f32
-        )
+    drift_x[...] = jnp.dot(
+        nodes_x[...].reshape(RX * MB, -1), pick_all[...], preferred_element_type=f32
+    )
     nodes_stage.wait_send()
     stage1.wait_recv()
     panel_modal = jnp.sum(h1[:, 0:1, :], axis=0)
@@ -479,10 +559,13 @@
             pltpu.VMEM((4, CX + 2, CY + 16, NZ), f32),
             pltpu.VMEM((4, CX + 2, CY + 16, NZ), f32),
             pltpu.VMEM((CX, CY, NZ), f32),
-            pltpu.VMEM((2, 2, 4, CY, NZ), bf16),
-            pltpu.VMEM((2, 2, 4, CY, NZ), bf16),
-            pltpu.VMEM((2, 2, 4, CX, NZ), f32),
-            pltpu.VMEM((2, 2, 4, CX, NZ), f32),
+            pltpu.VMEM((2, 2, 6, CY, NZ), bf16),
+            pltpu.VMEM((2, 2, 6, CY, NZ), bf16),
+            pltpu.VMEM((2, 2, 6, CX, NZ), f32),
+            pltpu.VMEM((2, 2, 6, CX, NZ), f32),
+            pltpu.VMEM((2, 2, CX, NZ), f32),
+            pltpu.VMEM((2, 4, NZ), f32),
+            pltpu.VMEM((2, 4, NZ), f32),
             pltpu.VMEM((SL, NZ), f32),
             pltpu.VMEM((128, NGX // RX * 128), bf16),
             pltpu.VMEM((16, NGX // RX * 128), bf16),
@@ -502,6 +585,8 @@
             pltpu.SemaphoreType.DMA((2, 4)),
             pltpu.SemaphoreType.DMA((2, 4)),
             pltpu.SemaphoreType.DMA((2, 4)),
+            pltpu.SemaphoreType.DMA((2,)),
+            pltpu.SemaphoreType.DMA((2,)),
             pltpu.SemaphoreType.DMA((7,)),
             pltpu.SemaphoreType.DMA((7,)),
             pltpu.SemaphoreType.REGULAR((2,)),

time: 47.7 us -> 46.4 us (0.973)
  Pallas kernels: 46.9 us -> 45.7 us
    pallas_call x1, Pallas kernels: 45.7 us -> 44.5 us  [body(): pl.pallas_call(kernel, out_shape=outs, in_specs=[hbm] * (3 + len(small)),...]
where the time goes in v4:
time: 46.4 us; the launch traced here: 46.3 us
  Pallas kernels  45.7 us (98%)
  between operations  0.65 us (1%)
    pallas_call x1, Pallas kernels, body(): pl.pallas_call(kernel, out_shape=outs, in_specs=[hbm] * (3 + len(small)),...  44.5 us
    pallas_call x1, Pallas kernels, body(): pl.pallas_call(write_out, out_shape=outs, in_specs=[vmem] * 4, out_specs=...  1.18 us

profile of v4, /device:TPU:1, one launch (start us, length us, event | category | flops | bytes accessed | tf_op | source)
XLA Modules:
  0.0 46.3 jit_solution(3198055392603557808)
XLA Ops:
  0.6 44.5 %shard_map.183 = (f32[3,8,48,256]{3,2,1,0:T(8,128)S(1)}, f32[8,48,256]{2,1,0:T(8,128)S(1)}, f32[2,32]{1,0:T(2,128)S(1)}, f32[1,64]{1,0:T(1,128)S(1)}) custom-call(f32[3,8,48,256]{3,2,1,0:T(8,128)} %vel_h.1, f32[8,48,256]{2,1,0:T(8,128)} %pre_h.1, f32[8,48,256]{2,1,0:T(8,128)} %vis_h.1, f32[1,256]{1,0:T(1,128)} %bitcast.16, f32[1,2048]{1,0:T(1,128)} %bitcast.15, ...), custom_call_target="tpu_custom_call" | custom-call | tf_op jit(solution)/shard_map/pallas_call | solution.py:553
  45.1 1.2 %shard_map.184 = (f32[3,8,48,256]{3,2,1,0:T(8,128)}, f32[8,48,256]{2,1,0:T(8,128)}, f32[2,32]{1,0:T(2,128)}, f32[1,64]{1,0:T(1,128)}) custom-call(f32[3,8,48,256]{3,2,1,0:T(8,128)S(1)} %get-tuple-element.12.refs_0_, f32[8,48,256]{2,1,0:T(8,128)S(1)} %get-tuple-element.13.refs_1_, f32[2,32]{1,0:T(2,128)S(1)} %get-tuple-element.14.refs_2_, ...), custom_call_target="tpu_custom_call" | custom-call | tf_op jit(solution)/shard_map/pallas_call | solution.py:598

commit v5 on v4

--- a/solution.py
+++ b/solution.py
@@ -245,21 +245,25 @@
     ring_b[ring, 3:4, :] = row_of(column_of(freq[...], MB), MB * ring)
     ring_b[ring, 4:5, :] = row_of(column_of(ratio[...], MB), MB * ring)
 
-    def spread(buf, me, count, sem_no, peer):
-        def send(k, carry):
+    def spread(buf, me, peers, sem_no):
+        for peer in peers:
             pltpu.make_async_remote_copy(
-                buf.at[me], buf.at[me], s_sem.at[sem_no], r_sem.at[sem_no], device_id=peer(k)
+                buf.at[me], buf.at[me], s_sem.at[sem_no], r_sem.at[sem_no], device_id=peer
             ).start()
-            return carry
-
-        lax.fori_loop(1, count, send, 0)
-        most = buf.at[pl.ds(0, count - 1)]
+        most = buf.at[pl.ds(0, len(peers))]
         return pltpu.make_async_remote_copy(
-            most, most, s_sem.at[sem_no], r_sem.at[sem_no], device_id=peer(1)
-        )
-
-    ring_stage = spread(ring_b, ring, RX, 0, x_peer)
-    damper_stage = spread(dampers_b, gy, NGY, 1, gy_peer)
+            most, most, s_sem.at[sem_no], r_sem.at[sem_no], device_id=peers[0]
+        )
+
+    def far_first(n):
+        return sorted(range(n), key=lambda k: -min(k, n - k))
+
+    z_peers = [z_peer(k) for k in far_first(nz)[:-1]]
+    gy_peers = [gy_peer(k) for k in far_first(NGY)[:-1]]
+    x_peers = [x_peer(k) for k in far_first(RX)[:-1]]
+
+    ring_stage = spread(ring_b, ring, x_peers, 0)
+    damper_stage = spread(dampers_b, gy, gy_peers, 1)
 
     parity = lax.rem(gx, 2)
     own_ids = column_of(panels[pl.ds(gx // 2, 1), :], SL, SL * parity)
@@ -308,6 +312,8 @@
             f1[3, x, rows, :] = pressure_tile(f0, x, t)
         return carry
 
+    shapes_x[ring] = shapes_t[...]
+    nodes_x[ring] = nodes_t[...]
     for c in hy1:
         c.wait_recv()
     corners = []
@@ -330,18 +336,11 @@
     lax.fori_loop(2, CX, first_layer, 0)
     for c in hx1:
         c.wait_recv()
+    shapes_stage = spread(shapes_x, ring, x_peers, 2)
     unpack_x(f0, 0, range(4))
     first_layer(1, 0)
     first_layer(CX, 0)
 
-    pack_x(f1, 1, (1, 2, 3))
-    pack_y(f1, 1, (1, 2, 3))
-    hx3 = [x_copy(1, 1, d, 1, 4) for d in range(2)]
-    hy3 = [y_copy(1, 1, d, 1, 4) for d in range(2)]
-    for c in hx3 + hy3:
-        c.start()
-    shapes_x[ring] = shapes_t[...]
-    shapes_stage = spread(shapes_x, ring, RX, 2, x_peer)
 
     for c in corners:
         c.wait_recv()
@@ -392,23 +391,15 @@
     ring_stage.wait_recv()
     g0[plane, 1:2, :] = jnp.sum(ring_b[:, 0:1, :], axis=0)
     pl.semaphore_wait(known.at[1], 2)
-    stage0 = spread(g0, plane, nz, 3, z_peer)
-    nodes_x[ring] = nodes_t[...]
-    nodes_stage = spread(nodes_x, ring, RX, 4, x_peer)
+    stage0 = spread(g0, plane, z_peers, 3)
+    nodes_stage = spread(nodes_x, ring, x_peers, 4)
+    pack_x(f1, 1, (1, 2, 3))
+    pack_y(f1, 1, (1, 2, 3))
+    hx3 = [x_copy(1, 1, d, 1, 4) for d in range(2)]
+    hy3 = [y_copy(1, 1, d, 1, 4) for d in range(2)]
     for c in hx3 + hy3:
-        c.wait_recv()
-    unpack_x(f1, 1, (1, 2, 3))
-    unpack_y(f1, 1, (1, 2, 3))
-
-    def second_velocity(x, carry):
-        for t in range(YT):
-            new = velocity_tile(f1, x, t)
-            for k in range(3):
-                vel_o[k, x - 1, 8 * t : 8 * t + 8, :] = new[k]
-        return carry
-
-    lax.fori_loop(1, CX + 1, second_velocity, 0)
-    for c in hx1 + hy1 + corners + hx3 + hy3 + [ring_stage, damper_stage]:
+        c.start()
+    for c in hx1 + hy1 + corners + [ring_stage, damper_stage]:
         c.wait_send()
     damper_stage.wait_recv()
 
@@ -465,11 +456,13 @@
     h1[spot, 2:3, :] = placed_half(stretch0)
     h1[spot, 3:4, :] = placed_half(hysteresis)
 
-    def plane_peer(k):
-        there = lax.rem(spot + k, RX * NGY)
-        return {"gx": plane * RX + there // NGY, "gy": lax.rem(there, NGY)}
-
-    stage1 = spread(h1, spot, RX * NGY, 5, plane_peer)
+    plane_peers = []
+    steps = [(a, b, c) for a in range(RX) for b in range(NGY // 2) for c in range(2)]
+    for a, b, c in sorted(steps, key=lambda k: -min(k[0], RX - k[0]) - min(k[1], NGY // 2 - k[1])):
+        if a or b or c:
+            there = 2 * lax.rem(gy // 2 + b, NGY // 2) + lax.rem(odd + c, 2)
+            plane_peers.append({"gx": plane * RX + lax.rem(ring + a, RX), "gy": there})
+    stage1 = spread(h1, spot, plane_peers, 5)
     stage0.wait_send()
     shapes_stage.wait_send()
     nodes_stage.wait_recv()
@@ -495,8 +488,23 @@
         g2[plane, j : j + 1, :] = jnp.sum(
             drift_x[:, j * 128 : (j + 1) * 128] * v1_column, axis=0, keepdims=True
         )
-    stage2 = spread(g2, plane, nz, 6, z_peer)
+    stage2 = spread(g2, plane, z_peers, 6)
     stage1.wait_send()
+    for c in hx3 + hy3:
+        c.wait_recv()
+    unpack_x(f1, 1, (1, 2, 3))
+    unpack_y(f1, 1, (1, 2, 3))
+
+    def second_velocity(x, carry):
+        for t in range(YT):
+            new = velocity_tile(f1, x, t)
+            for k in range(3):
+                vel_o[k, x - 1, 8 * t : 8 * t + 8, :] = new[k]
+        return carry
+
+    lax.fori_loop(1, CX + 1, second_velocity, 0)
+    for c in hx3 + hy3:
+        c.wait_send()
     stage2.wait_recv()
     rate_all = jnp.sum(g2[...], axis=0)
     stretch_all = stretch_all + modal_step * rate_all

time: 46.4 us -> 45.1 us (0.972)
  Pallas kernels: 45.7 us -> 44.3 us
    pallas_call x1, Pallas kernels: 44.5 us -> 43.1 us  [body(): pl.pallas_call(kernel, out_shape=outs, in_specs=[hbm] * (3 + len(small)),...]
where the time goes in v5:
time: 45.1 us; the launch traced here: 45 us
  Pallas kernels  44.3 us (98%)
  between operations  0.65 us (1%)
    pallas_call x1, Pallas kernels, body(): pl.pallas_call(kernel, out_shape=outs, in_specs=[hbm] * (3 + len(small)),...  43.1 us
    pallas_call x1, Pallas kernels, body(): pl.pallas_call(write_out, out_shape=outs, in_specs=[vmem] * 4, out_specs=...  1.18 us

profile of v5, /device:TPU:1, one launch (start us, length us, event | category | flops | bytes accessed | tf_op | source)
XLA Modules:
  0.0 45.0 jit_solution(5220795959027721414)
XLA Ops:
  0.6 43.1 %shard_map.183 = (f32[3,8,48,256]{3,2,1,0:T(8,128)S(1)}, f32[8,48,256]{2,1,0:T(8,128)S(1)}, f32[2,32]{1,0:T(2,128)S(1)}, f32[1,64]{1,0:T(1,128)S(1)}) custom-call(f32[3,8,48,256]{3,2,1,0:T(8,128)} %vel_h.1, f32[8,48,256]{2,1,0:T(8,128)} %pre_h.1, f32[8,48,256]{2,1,0:T(8,128)} %vis_h.1, f32[1,256]{1,0:T(1,128)} %bitcast.16, f32[1,2048]{1,0:T(1,128)} %bitcast.15, ...), custom_call_target="tpu_custom_call" | custom-call | tf_op jit(solution)/shard_map/pallas_call | solution.py:561
  43.8 1.2 %shard_map.184 = (f32[3,8,48,256]{3,2,1,0:T(8,128)}, f32[8,48,256]{2,1,0:T(8,128)}, f32[2,32]{1,0:T(2,128)}, f32[1,64]{1,0:T(1,128)}) custom-call(f32[3,8,48,256]{3,2,1,0:T(8,128)S(1)} %get-tuple-element.12.refs_0_, f32[8,48,256]{2,1,0:T(8,128)S(1)} %get-tuple-element.13.refs_1_, f32[2,32]{1,0:T(2,128)S(1)} %get-tuple-element.14.refs_2_, ...), custom_call_target="tpu_custom_call" | custom-call | tf_op jit(solution)/shard_map/pallas_call | solution.py:606

commit v6 on v5

--- a/solution.py
+++ b/solution.py
@@ -392,13 +392,6 @@
     g0[plane, 1:2, :] = jnp.sum(ring_b[:, 0:1, :], axis=0)
     pl.semaphore_wait(known.at[1], 2)
     stage0 = spread(g0, plane, z_peers, 3)
-    nodes_stage = spread(nodes_x, ring, x_peers, 4)
-    pack_x(f1, 1, (1, 2, 3))
-    pack_y(f1, 1, (1, 2, 3))
-    hx3 = [x_copy(1, 1, d, 1, 4) for d in range(2)]
-    hy3 = [y_copy(1, 1, d, 1, 4) for d in range(2)]
-    for c in hx3 + hy3:
-        c.start()
     for c in hx1 + hy1 + corners + [ring_stage, damper_stage]:
         c.wait_send()
     damper_stage.wait_recv()
@@ -423,6 +416,7 @@
     q0_row, v0_row, omega, zeta = (jnp.sum(ring_b[:, r : r + 1, :], axis=0) for r in range(1, 5))
 
     shapes_stage.wait_recv()
+    nodes_stage = spread(nodes_x, ring, x_peers, 4)
     stage0.wait_recv()
     sub16 = lax.broadcasted_iota(jnp.int32, (16, 128), 0)
     for i in range(nz):
@@ -469,6 +463,12 @@
     drift_x[...] = jnp.dot(
         nodes_x[...].reshape(RX * MB, -1), pick_all[...], preferred_element_type=f32
     )
+    pack_x(f1, 1, (1, 2, 3))
+    pack_y(f1, 1, (1, 2, 3))
+    hx3 = [x_copy(1, 1, d, 1, 4) for d in range(2)]
+    hy3 = [y_copy(1, 1, d, 1, 4) for d in range(2)]
+    for c in hx3 + hy3:
+        c.start()
     nodes_stage.wait_send()
     stage1.wait_recv()
     panel_modal = jnp.sum(h1[:, 0:1, :], axis=0)

time: 45.1 us -> 43.9 us (0.973)
  Pallas kernels: 44.3 us -> 43.1 us
    pallas_call x1, Pallas kernels: 43.1 us -> 41.9 us  [body(): pl.pallas_call(kernel, out_shape=outs, in_specs=[hbm] * (3 + len(small)),...]
where the time goes in v6:
time: 43.9 us; the launch traced here: 43.8 us
  Pallas kernels  43.1 us (98%)
  between operations  0.65 us (1%)
    pallas_call x1, Pallas kernels, body(): pl.pallas_call(kernel, out_shape=outs, in_specs=[hbm] * (3 + len(small)),...  41.9 us
    pallas_call x1, Pallas kernels, body(): pl.pallas_call(write_out, out_shape=outs, in_specs=[vmem] * 4, out_specs=...  1.18 us

profile of v6, /device:TPU:1, one launch (start us, length us, event | category | flops | bytes accessed | tf_op | source)
XLA Modules:
  0.0 43.8 jit_solution(12475030298766747685)
XLA Ops:
  0.6 41.9 %shard_map.183 = (f32[3,8,48,256]{3,2,1,0:T(8,128)S(1)}, f32[8,48,256]{2,1,0:T(8,128)S(1)}, f32[2,32]{1,0:T(2,128)S(1)}, f32[1,64]{1,0:T(1,128)S(1)}) custom-call(f32[3,8,48,256]{3,2,1,0:T(8,128)} %vel_h.1, f32[8,48,256]{2,1,0:T(8,128)} %pre_h.1, f32[8,48,256]{2,1,0:T(8,128)} %vis_h.1, f32[1,256]{1,0:T(1,128)} %bitcast.16, f32[1,2048]{1,0:T(1,128)} %bitcast.15, ...), custom_call_target="tpu_custom_call" | custom-call | tf_op jit(solution)/shard_map/pallas_call | solution.py:561
  42.6 1.2 %shard_map.184 = (f32[3,8,48,256]{3,2,1,0:T(8,128)}, f32[8,48,256]{2,1,0:T(8,128)}, f32[2,32]{1,0:T(2,128)}, f32[1,64]{1,0:T(1,128)}) custom-call(f32[3,8,48,256]{3,2,1,0:T(8,128)S(1)} %get-tuple-element.12.refs_0_, f32[8,48,256]{2,1,0:T(8,128)S(1)} %get-tuple-element.13.refs_1_, f32[2,32]{1,0:T(2,128)S(1)} %get-tuple-element.14.refs_2_, ...), custom_call_target="tpu_custom_call" | custom-call | tf_op jit(solution)/shard_map/pallas_call | solution.py:606

commit v7 on v6

--- a/solution.py
+++ b/solution.py
@@ -333,10 +333,10 @@
     unpack_y(f0, 0, range(4))
     pl.semaphore_wait(known.at[0], 2 + len(ring_peers))
     tell(1, [z_peer(4), z_peer(nz - 4)])
+    shapes_stage = spread(shapes_x, ring, x_peers, 2)
     lax.fori_loop(2, CX, first_layer, 0)
     for c in hx1:
         c.wait_recv()
-    shapes_stage = spread(shapes_x, ring, x_peers, 2)
     unpack_x(f0, 0, range(4))
     first_layer(1, 0)
     first_layer(CX, 0)

time: 43.9 us -> 44.8 us (1.021)
  Pallas kernels: 43.1 us -> 44 us
    pallas_call x1, Pallas kernels: 41.9 us -> 42.8 us  [body(): pl.pallas_call(kernel, out_shape=outs, in_specs=[hbm] * (3 + len(small)),...]
where the time goes in v7:
time: 44.8 us; the launch traced here: 44.6 us
  Pallas kernels  44 us (98%)
  between operations  0.65 us (1%)
    pallas_call x1, Pallas kernels, body(): pl.pallas_call(kernel, out_shape=outs, in_specs=[hbm] * (3 + len(small)),...  42.8 us
    pallas_call x1, Pallas kernels, body(): pl.pallas_call(write_out, out_shape=outs, in_specs=[vmem] * 4, out_specs=...  1.18 us

profile of v7, /device:TPU:1, one launch (start us, length us, event | category | flops | bytes accessed | tf_op | source)
XLA Modules:
  0.0 44.6 jit_solution(15804807981850033129)
XLA Ops:
  0.6 42.8 %shard_map.183 = (f32[3,8,48,256]{3,2,1,0:T(8,128)S(1)}, f32[8,48,256]{2,1,0:T(8,128)S(1)}, f32[2,32]{1,0:T(2,128)S(1)}, f32[1,64]{1,0:T(1,128)S(1)}) custom-call(f32[3,8,48,256]{3,2,1,0:T(8,128)} %vel_h.1, f32[8,48,256]{2,1,0:T(8,128)} %pre_h.1, f32[8,48,256]{2,1,0:T(8,128)} %vis_h.1, f32[1,256]{1,0:T(1,128)} %bitcast.16, f32[1,2048]{1,0:T(1,128)} %bitcast.15, ...), custom_call_target="tpu_custom_call" | custom-call | tf_op jit(solution)/shard_map/pallas_call | solution.py:561
  43.5 1.2 %shard_map.184 = (f32[3,8,48,256]{3,2,1,0:T(8,128)}, f32[8,48,256]{2,1,0:T(8,128)}, f32[2,32]{1,0:T(2,128)}, f32[1,64]{1,0:T(1,128)}) custom-call(f32[3,8,48,256]{3,2,1,0:T(8,128)S(1)} %get-tuple-element.12.refs_0_, f32[8,48,256]{2,1,0:T(8,128)S(1)} %get-tuple-element.13.refs_1_, f32[2,32]{1,0:T(2,128)S(1)} %get-tuple-element.14.refs_2_, ...), custom_call_target="tpu_custom_call" | custom-call | tf_op jit(solution)/shard_map/pallas_call | solution.py:606
